TPU v7x, 256 devices: a whole 4x4x8 slice. The times are simulated.
256 devices in a mesh: blk: 16 (over z, core), head: 4 (over x), dp: 4 (over y).
Axes of the slice: x: 4, y: 4, z: 8, core: 2. Of those that a mesh axis runs over, the one named last changes fastest.
Arguments:
- hidden: bfloat16 [49152, 3072], P(('dp', 'blk', 'head')), parts along dimension 0, may hold values from -36 to 36
- qkv_weight: bfloat16 [3, 3072, 1536], P(None, None, 'head'), may hold values from -0.109375 to 0.109375
- qkv_bias: bfloat16 [3, 1536], P(None, 'head'), may hold values from -3 to 3
- norm_gains: float32 [2, 128], replicated, may hold values from 0.25 to 1.75
- tile_lists: int32 [128, 12], P('dp'), parts along dimension 0, may hold values from 0 to 31, as said below
- tile_counts: int32 [128], P('dp'), parts along dimension 0, may hold values from 1 to 12
Outputs:
- attended: bfloat16 [49152, 1536], P(('dp', 'blk', 'head')), parts along dimension 0
There are 4 independent parts, one for each index of `dp`. A program takes and returns all parts, laid end to end along the dimension named above; an argument that names none is the same for every part. Nothing has to cross between parts.
Inputs may be any that keep to these rules, and one draw needn't show every extreme that they name: `tile_lists`: entries 0 to tile_counts[a] - 1 of row a name distinct tiles, tile a among them; later entries are arbitrary tile indices.
All inputs are finite; a program needn't handle non-finite values.
Results may differ from a plain program's by a relative error of at most 0.0034.
Values may be sent and summed in bfloat16 or wider, within the bound.
A program may use at most 64 MiB of HBM per device.

v0:
```python
import jax
import jax.numpy as jnp
from jax import lax
from jax.sharding import PartitionSpec as P

HD = 128
TILE = 384


def shifted(block, axis, distance):
    devices = range(lax.axis_size(axis))
    route = [(i - distance, i) for i in devices if i - distance in devices]
    return lax.ppermute(block, axis, route)


def norm_heads(values, gain, heads):
    rows = values.shape[0]
    split = values.reshape(rows, heads, HD)
    mean_sq = jnp.mean(split * split, axis=-1, keepdims=True)
    return (split * lax.rsqrt(mean_sq + 1e-06) * gain).reshape(rows, heads * HD)


def tile_mask(lists, counts, start, rows):
    key_tile = (start + jnp.arange(rows, dtype=jnp.int32)) // TILE
    live = jnp.arange(lists.shape[1], dtype=jnp.int32)[None, :] < counts[:, None]
    hits = (lists[:, :, None] == key_tile[None, None, :]) & live[:, :, None]
    return jnp.any(hits, axis=1)


def tile_terms(query, keys, values, mask, heads):
    count_q = query.shape[0]
    rows = keys.shape[0]
    query_h = query.reshape(count_q, heads, HD)
    keys_h = keys.reshape(rows, heads, HD)
    values_h = values.reshape(rows, heads, HD)
    score = jnp.einsum(
        "qhd,khd->hqk", query_h, keys_h, preferred_element_type=jnp.float32
    ) * HD ** (-0.5)
    score = score.reshape(heads, count_q // TILE, TILE, rows)
    weights = jnp.where(mask[None, :, None, :], jnp.exp(score), jnp.float32(0.0)).reshape(
        heads, count_q, rows
    )
    sums = jnp.sum(weights, axis=-1)
    terms = jnp.einsum(
        "hqk,khd->qhd", weights.astype(jnp.bfloat16), values_h, preferred_element_type=jnp.float32
    )
    return (sums, terms.reshape(count_q, heads * HD))


def add_block(state, query, lists, counts, keys, values, start, heads):
    total, numer = state
    mask = tile_mask(lists, counts, start, keys.shape[0])
    sums, terms = tile_terms(query, keys, values, mask, heads)
    return (total + sums, numer + terms)


def attend(state, query, lists, counts, keys, values, start, heads):
    return add_block(state, query, lists, counts, keys, values, start, heads)


def shards(hidden, qkv_weight, qkv_bias, norm_gains, tile_lists, tile_counts):
    heads = qkv_weight.shape[2] // HD
    piece = lax.all_gather(hidden, "head", axis=0, tiled=True)
    made = [
        jnp.dot(piece, qkv_weight[j], preferred_element_type=jnp.float32)
        + qkv_bias[j].astype(jnp.float32)
        for j in range(3)
    ]
    query_part = norm_heads(made[0], norm_gains[0], heads)
    key_part = norm_heads(made[1], norm_gains[1], heads)
    stacked = jnp.stack([query_part, key_part, made[2]]).astype(jnp.bfloat16)
    query = stacked[0]
    key_value = stacked[1:3]
    rows_blk = query.shape[0]
    tiles_here = rows_blk // TILE
    place = lax.axis_index("blk")
    lists = lax.dynamic_slice_in_dim(tile_lists, place * tiles_here, tiles_here, 0)
    counts = lax.dynamic_slice_in_dim(tile_counts, place * tiles_here, tiles_here, 0)
    state = (
        jnp.zeros((heads, rows_blk), jnp.float32),
        jnp.zeros((rows_blk, heads * HD), jnp.float32),
    )
    key_group = lists // tiles_here
    live = jnp.arange(lists.shape[1], dtype=jnp.int32)[None, :] < counts[:, None]
    ahead = jnp.max(jnp.where(live, key_group - place, 0))
    behind = jnp.max(jnp.where(live, place - key_group, 0))
    farthest = lax.pmax(jnp.stack([ahead, behind]), "blk")
    state = attend(state, query, lists, counts, key_value[0], key_value[1], place * rows_blk, heads)

    def turn(step, carry):
        current, above, below = carry
        above = shifted(above, "blk", -1)
        below = shifted(below, "blk", 1)
        current = attend(
            current, query, lists, counts, above[0], above[1], (place + step + 1) * rows_blk, heads
        )
        current = attend(
            current, query, lists, counts, below[0], below[1], (place - step - 1) * rows_blk, heads
        )
        return (current, above, below)

    steps = jnp.maximum(farthest[0], farthest[1])
    state, unused_above, unused_below = lax.fori_loop(0, steps, turn, (state, key_value, key_value))
    total, numer = state
    attended = (
        (numer.reshape(rows_blk, heads, HD) / total.T[:, :, None])
        .reshape(rows_blk, heads * HD)
        .astype(jnp.bfloat16)
    )
    return lax.all_to_all(attended, "head", split_axis=0, concat_axis=1, tiled=True)


def solution(mesh):
    return jax.shard_map(
        shards,
        mesh=mesh,
        in_specs=(
            P(("dp", "blk", "head"), None),
            P(None, None, "head"),
            P(None, "head"),
            P(),
            P("dp", None),
            P("dp"),
        ),
        out_specs=P(("dp", "blk", "head"), None),
        check_vma=False,
    )
```

profile of v0, /device:TPU:1, one launch (start us, length us, event | category | flops | bytes accessed | tf_op | source)
XLA Modules:
  0.0 198.1 jit_solution(13299230233405282443)
XLA Ops:
  8.9 1.3 pad_add_fusion
  10.2 14.7 %pmax.7 = s32[2]{0:T(128)S(1)} all-reduce(s32[2]{0:T(128)S(1)} %pad_add_fusion), channel_id=1, replica_groups=mesh['blk'=16,'head'=4,'dp'=4] {'blk'}, use_global_device_ids=true, to_apply=%region_6.7 | all-reduce | flops 2 | bytes 16 | tf_op jit(solution)/shard_map/pmax | solution.py:87
  25.3 1.6 copy.56
  29.8 38.1 %all-gather.2.cloned.1.call-done = bf16[768,3072]{1,0:T(8,128)(2,1)} async-done(((bf16[192,3072]{1,0:T(8,128)(2,1)}), bf16[768,3072]{1,0:T(8,128)(2,1)}) %all-gather.2.cloned.1.call-update) | async-done | bytes 4718608 | tf_op jit(solution)/shard_map/all_gather | solution.py:63
  67.9 5.1 %fusion.60 = (f32[768,384]{0,1:T(8,128)S(1)}, f32[768,384]{0,1:T(8,128)S(1)}) fusion(f32[384]{0:T(512)S(1)} %get-tuple-element.181, bf16[768,3072]{1,0:T(8,128)(2,1)} %all-gather.2.cloned.1.call-done, bf16[3,3072,384]{2,1,0:T(8,128)(2,1)} %param.9), kind=kOutput, calls=%fused_computation.93 | convolution fusion | flops 1812529152 | bytes 9438720 | tf_op jit(solution)/shard_map/dot_general | solution.py:65
  73.7 5.1 %fusion.59 = (f32[768,384]{0,1:T(8,128)S(1)}, f32[768,384]{0,1:T(8,128)S(1)}) fusion(f32[384]{0:T(512)} %get-tuple-element.180, bf16[768,3072]{1,0:T(8,128)(2,1)} %all-gather.2.cloned.1.call-done, bf16[3,3072,384]{2,1,0:T(8,128)(2,1)} %param.9), kind=kOutput, calls=%fused_computation.92 | convolution fusion | flops 1812529152 | bytes 9439232 | tf_op jit(solution)/shard_map/dot_general | solution.py:65
  81.1 5.1 %fusion.45 = bf16[768,384]{0,1:T(8,128)(2,1)S(1)} fusion(bf16[768,3072]{1,0:T(8,128)(2,1)} %all-gather.2.cloned.1.call-done, bf16[3,3072,384]{2,1,0:T(8,128)(2,1)} %param.9, f32[384]{0:T(512)} %get-tuple-element.179), kind=kOutput, calls=%fused_computation.53 | convolution fusion | flops 1812529152 | bytes 7669760 | tf_op jit(solution)/shard_map/dot_general | solution.py:65
  86.2 1.1 pad_maximum_fusion
  87.3 2.5 %copy.81 = bf16[2,768,384]{1,2,0:T(8,128)(2,1)} copy(bf16[2,768,384]{1,2,0:T(8,128)(2,1)} %pad_maximum_fusion) | data formatting | bytes 2359296
  90.0 2.5 %fusion.21 = (f32[3,768]{1,0:T(4,128)}, f32[3,768,768]{1,2,0:T(8,128)S(1)}) fusion(pred[768,768]{0,1:T(8,128)(4,1)S(1)} %copy-done.4, bf16[768,3,128]{0,2,1:T(8,128)(2,1)S(1)} %bitcast.138, bf16[768,3,128]{0,2,1:T(8,128)(2,1)S(1)} %bitcast.135), kind=kOutput, calls=%fused_computation.36 | convolution fusion | flops 458290944 | bytes 8856576 | tf_op jit(solution)/shard_map/qhd,khd->hqk/dot_general | solution.py:36
  92.5 2.6 %fusion.22 = f32[3,128,768]{2,1,0:T(8,128)} fusion(bf16[768,3,128]{0,2,1:T(8,128)(2,1)S(1)} %bitcast.143, f32[3,768,768]{1,2,0:T(8,128)S(1)} %get-tuple-element.223, pred[768,768]{0,1:T(8,128)(4,1)S(1)} %copy-done.4), kind=kOutput, calls=%fused_computation.37 | convolution fusion | flops 458293248 | bytes 9437184 | tf_op jit(solution)/shard_map/hqk,khd->qhd/dot_general | solution.py:44
  95.1 83.5 %while.19 = (s32[]{:T(128)}, f32[3,768]{1,0:T(4,128)}, f32[768,384]{0,1:T(8,128)}, bf16[2,768,384]{1,2,0:T(8,128)(2,1)}, bf16[2,768,384]{1,2,0:T(8,128)(2,1)}, /...) while((s32[]{:T(128)}, f32[3,768]{1,0:T(4,128)}, ...), condition=%wide.region_12.13_spmd, body=%wide.region_7.12_spmd.sunk | while | flops 1833884160 | bytes 78004824 | solution.py:103
  95.1 2.7 %collective-permute-start.1 = (bf16[2,768,384]{1,2,0:T(8,128)(2,1)}, bf16[2,768,384]{1,2,0:T(8,128)(2,1)S(1)}, u32[]{:S(2)}, u32[]{:S(2)}) collective-permute-start(bf16[2,768,384]{1,2,0:T(8,128)(2,1)} %get-tuple-element.328), channel_id=1, source_target_pairs={{16,0},{32,16},{48,32},{64,48},{80,64},{96,80},{112,96},{128,112},... | collective-permute-start | bytes 3538952 | tf_op jit(solution)/shard_map/while/body/ppermute | solution.py:13
  97.8 3.1 %collective-permute-start = (bf16[2,768,384]{1,2,0:T(8,128)(2,1)}, bf16[2,768,384]{1,2,0:T(8,128)(2,1)S(1)}, u32[]{:S(2)}, u32[]{:S(2)}) collective-permute-start(bf16[2,768,384]{1,2,0:T(8,128)(2,1)} %get-tuple-element.329), channel_id=1, source_target_pairs={{0,16},{16,32},{32,48},{48,64},{64,80},{80,96},{96,112},{112,128},... | collective-permute-start | bytes 3538952 | tf_op jit(solution)/shard_map/while/body/ppermute | solution.py:13
  101.3 1.6 copy.76
  103.1 1.0 copy.75
  104.1 9.0 %collective-permute-done.1 = bf16[2,768,384]{1,2,0:T(8,128)(2,1)S(1)} collective-permute-done((bf16[2,768,384]{1,2,0:T(8,128)(2,1)}, bf16[2,768,384]{1,2,0:T(8,128)(2,1)S(1)}, u32[]{:S(2)}, u32[]{:S(2)}) %collective-permute-start.1) | collective-permute-done | bytes 1179680 | tf_op jit(solution)/shard_map/while/body/ppermute | solution.py:13
  113.2 1.9 fusion.98
  115.1 1.6 fusion.100
  116.8 1.9 fusion.96
  118.7 1.5 fusion.99
  121.0 1.0 copy.90
  122.0 1.0 copy.91
  123.1 1.9 collective-permute-start.1
  125.0 3.6 %collective-permute-start = (bf16[2,768,384]{1,2,0:T(8,128)(2,1)}, bf16[2,768,384]{1,2,0:T(8,128)(2,1)S(1)}, u32[]{:S(2)}, u32[]{:S(2)}) collective-permute-start(bf16[2,768,384]{1,2,0:T(8,128)(2,1)} %get-tuple-element.329), channel_id=1, source_target_pairs={{0,16},{16,32},{32,48},{48,64},{64,80},{80,96},{96,112},{112,128},... | collective-permute-start | bytes 3538952 | tf_op jit(solution)/shard_map/while/body/ppermute | solution.py:13
  129.1 1.6 copy.76
  130.8 1.0 copy.75
  131.8 9.0 %collective-permute-done.1 = bf16[2,768,384]{1,2,0:T(8,128)(2,1)S(1)} collective-permute-done((bf16[2,768,384]{1,2,0:T(8,128)(2,1)}, bf16[2,768,384]{1,2,0:T(8,128)(2,1)S(1)}, u32[]{:S(2)}, u32[]{:S(2)}) %collective-permute-start.1) | collective-permute-done | bytes 1179680 | tf_op jit(solution)/shard_map/while/body/ppermute | solution.py:13
  140.9 1.9 fusion.98
  142.9 1.6 fusion.100
  144.6 1.9 fusion.96
  146.5 1.5 fusion.99
  148.7 1.0 copy.90
  149.8 1.0 copy.91
  150.8 1.9 collective-permute-start.1
  152.7 3.6 %collective-permute-start = (bf16[2,768,384]{1,2,0:T(8,128)(2,1)}, bf16[2,768,384]{1,2,0:T(8,128)(2,1)S(1)}, u32[]{:S(2)}, u32[]{:S(2)}) collective-permute-start(bf16[2,768,384]{1,2,0:T(8,128)(2,1)} %get-tuple-element.329), channel_id=1, source_target_pairs={{0,16},{16,32},{32,48},{48,64},{64,80},{80,96},{96,112},{112,128},... | collective-permute-start | bytes 3538952 | tf_op jit(solution)/shard_map/while/body/ppermute | solution.py:13
  156.8 1.6 copy.76
  158.5 1.0 copy.75
  159.6 9.0 %collective-permute-done.1 = bf16[2,768,384]{1,2,0:T(8,128)(2,1)S(1)} collective-permute-done((bf16[2,768,384]{1,2,0:T(8,128)(2,1)}, bf16[2,768,384]{1,2,0:T(8,128)(2,1)S(1)}, u32[]{:S(2)}, u32[]{:S(2)}) %collective-permute-start.1) | collective-permute-done | bytes 1179680 | tf_op jit(solution)/shard_map/while/body/ppermute | solution.py:13
  168.7 1.9 fusion.98
  170.6 1.6 fusion.100
  172.3 1.9 fusion.96
  174.2 1.5 fusion.99
  176.5 1.0 copy.90
  177.5 1.0 copy.91
  178.6 1.4 fusion.48
  180.2 10.2 %all_to_all.19 = bf16[4,192,384]{2,1,0:T(8,128)(2,1)S(1)} all-to-all(bf16[4,192,384]{2,1,0:T(8,128)(2,1)S(1)} %bitcast.132), channel_id=1, replica_groups=mesh['blk'=16,'head'=4,'dp'=4] {'head'}, dimensions={0} | all-to-all | bytes 1179648 | tf_op jit(solution)/shard_map/all_to_all | solution.py:110
  190.4 0.9 copy.72
  (101 shorter events, 12.1 us)
Async XLA Ops:
  6.5 0.7 copy-start
  6.5 22.1 %copy-start.9 = (bf16[3,384]{1,0:T(4,128)(2,1)S(1)}, bf16[3,384]{1,0:T(4,128)(2,1)}, u32[]{:S(2)}) copy-start(bf16[3,384]{1,0:T(4,128)(2,1)} %param.10) | copy-start | bytes 6916
  6.5 22.7 %copy-start.10 = (f32[2,128]{1,0:T(2,128)S(1)}, f32[2,128]{1,0:T(2,128)}, u32[]{:S(2)}) copy-start(f32[2,128]{1,0:T(2,128)} %param.11) | copy-start | bytes 3076
  6.5 61.3 %all-gather.2.cloned.1.call-start = ((), (), s32[]{:S(2)}) async-start(), calls=%async_computation.1 | async-start | bytes 5898240 | tf_op jit(solution)/shard_map/all_gather | solution.py:63
  8.2 16.8 %copy-start.11 = (s32[2]{0:T(128)}, s32[2]{0:T(128)S(1)}, u32[]{:S(2)}) copy-start(s32[2]{0:T(128)S(1)} %dynamic_slice.7) | copy-start | bytes 28
  87.3 2.7 %copy-start.4 = (pred[768,768]{0,1:T(8,128)(4,1)S(1)}, pred[768,768]{0,1:T(8,128)(4,1)}, u32[]{:S(2)}) copy-start(pred[768,768]{0,1:T(8,128)(4,1)} %copy.56) | copy-start | bytes 1769476
  90.0 2.5 %copy-start.5 = (bf16[768,384]{0,1:T(8,128)(2,1)}, bf16[768,384]{0,1:T(8,128)(2,1)S(1)}, u32[]{:S(2)}) copy-start(bf16[768,384]{0,1:T(8,128)(2,1)S(1)} %fusion.52) | copy-start | bytes 1769476
  92.5 2.6 %copy-start.12 = (s32[2]{0:T(128)S(1)}, s32[2]{0:T(128)}, u32[]{:S(2)}) copy-start(s32[2]{0:T(128)} %copy-done.11) | copy-start | bytes 28
  95.1 18.0 %collective-permute-start.1 = (bf16[2,768,384]{1,2,0:T(8,128)(2,1)}, bf16[2,768,384]{1,2,0:T(8,128)(2,1)S(1)}, u32[]{:S(2)}, u32[]{:S(2)}) collective-permute-start(bf16[2,768,384]{1,2,0:T(8,128)(2,1)} %get-tuple-element.328), channel_id=1, source_target_pairs={{16,0},{32,16},{48,32},{64,48},{80,64},{96,80},{112,96},{128,112},... | collective-permute-start | bytes 3538952 | tf_op jit(solution)/shard_map/while/body/ppermute | solution.py:13
  97.8 18.9 %collective-permute-start = (bf16[2,768,384]{1,2,0:T(8,128)(2,1)}, bf16[2,768,384]{1,2,0:T(8,128)(2,1)S(1)}, u32[]{:S(2)}, u32[]{:S(2)}) collective-permute-start(bf16[2,768,384]{1,2,0:T(8,128)(2,1)} %get-tuple-element.329), channel_id=1, source_target_pairs={{0,16},{16,32},{32,48},{48,64},{64,80},{80,96},{96,112},{112,128},... | collective-permute-start | bytes 3538952 | tf_op jit(solution)/shard_map/while/body/ppermute | solution.py:13
  104.1 9.1 %copy-start.3 = (pred[768,768]{0,1:T(8,128)(4,1)S(1)}, pred[768,768]{0,1:T(8,128)(4,1)}, u32[]{:S(2)}) copy-start(pred[768,768]{0,1:T(8,128)(4,1)} %copy.76) | copy-start | bytes 1769476 | tf_op jit(solution)/shard_map/while
  104.1 9.1 %copy-start.6 = (bf16[1,768,384]{1,2,0:T(8,128)(2,1)S(1)}, bf16[1,768,384]{1,2,0:T(8,128)(2,1)}, u32[]{:S(2)}) copy-start(bf16[1,768,384]{1,2,0:T(8,128)(2,1)} %get-tuple-element.347) | copy-start | bytes 1769476 | tf_op jit(solution)/shard_map/while
  118.7 1.6 copy-start.1
  120.3 0.7 copy-start.7
  120.6 2.5 %copy-start.2 = (f32[768,384]{0,1:T(8,128)}, f32[768,384]{0,1:T(8,128)S(1)}, u32[]{:S(2)}) copy-start(f32[768,384]{0,1:T(8,128)S(1)} %bitcast_add_fusion.3) | copy-start | bytes 3538948 | tf_op jit(solution)/shard_map/while
  121.0 2.1 %copy-start.8 = (f32[3,768]{1,0:T(4,128)}, f32[3,768]{1,0:T(4,128)S(1)}, u32[]{:S(2)}) copy-start(f32[3,768]{1,0:T(4,128)S(1)} %add_add_fusion.2) | copy-start | bytes 27652 | tf_op jit(solution)/shard_map/while
  123.1 17.7 %collective-permute-start.1 = (bf16[2,768,384]{1,2,0:T(8,128)(2,1)}, bf16[2,768,384]{1,2,0:T(8,128)(2,1)S(1)}, u32[]{:S(2)}, u32[]{:S(2)}) collective-permute-start(bf16[2,768,384]{1,2,0:T(8,128)(2,1)} %get-tuple-element.328), channel_id=1, source_target_pairs={{16,0},{32,16},{48,32},{64,48},{80,64},{96,80},{112,96},{128,112},... | collective-permute-start | bytes 3538952 | tf_op jit(solution)/shard_map/while/body/ppermute | solution.py:13
  125.0 19.4 %collective-permute-start = (bf16[2,768,384]{1,2,0:T(8,128)(2,1)}, bf16[2,768,384]{1,2,0:T(8,128)(2,1)S(1)}, u32[]{:S(2)}, u32[]{:S(2)}) collective-permute-start(bf16[2,768,384]{1,2,0:T(8,128)(2,1)} %get-tuple-element.329), channel_id=1, source_target_pairs={{0,16},{16,32},{32,48},{48,64},{64,80},{80,96},{96,112},{112,128},... | collective-permute-start | bytes 3538952 | tf_op jit(solution)/shard_map/while/body/ppermute | solution.py:13
  131.8 9.1 %copy-start.3 = (pred[768,768]{0,1:T(8,128)(4,1)S(1)}, pred[768,768]{0,1:T(8,128)(4,1)}, u32[]{:S(2)}) copy-start(pred[768,768]{0,1:T(8,128)(4,1)} %copy.76) | copy-start | bytes 1769476 | tf_op jit(solution)/shard_map/while
  131.8 9.1 %copy-start.6 = (bf16[1,768,384]{1,2,0:T(8,128)(2,1)S(1)}, bf16[1,768,384]{1,2,0:T(8,128)(2,1)}, u32[]{:S(2)}) copy-start(bf16[1,768,384]{1,2,0:T(8,128)(2,1)} %get-tuple-element.347) | copy-start | bytes 1769476 | tf_op jit(solution)/shard_map/while
  146.5 1.6 copy-start.1
  148.0 0.7 copy-start.7
  148.4 2.5 %copy-start.2 = (f32[768,384]{0,1:T(8,128)}, f32[768,384]{0,1:T(8,128)S(1)}, u32[]{:S(2)}) copy-start(f32[768,384]{0,1:T(8,128)S(1)} %bitcast_add_fusion.3) | copy-start | bytes 3538948 | tf_op jit(solution)/shard_map/while
  148.7 2.1 %copy-start.8 = (f32[3,768]{1,0:T(4,128)}, f32[3,768]{1,0:T(4,128)S(1)}, u32[]{:S(2)}) copy-start(f32[3,768]{1,0:T(4,128)S(1)} %add_add_fusion.2) | copy-start | bytes 27652 | tf_op jit(solution)/shard_map/while
  150.8 17.7 %collective-permute-start.1 = (bf16[2,768,384]{1,2,0:T(8,128)(2,1)}, bf16[2,768,384]{1,2,0:T(8,128)(2,1)S(1)}, u32[]{:S(2)}, u32[]{:S(2)}) collective-permute-start(bf16[2,768,384]{1,2,0:T(8,128)(2,1)} %get-tuple-element.328), channel_id=1, source_target_pairs={{16,0},{32,16},{48,32},{64,48},{80,64},{96,80},{112,96},{128,112},... | collective-permute-start | bytes 3538952 | tf_op jit(solution)/shard_map/while/body/ppermute | solution.py:13
  152.7 19.4 %collective-permute-start = (bf16[2,768,384]{1,2,0:T(8,128)(2,1)}, bf16[2,768,384]{1,2,0:T(8,128)(2,1)S(1)}, u32[]{:S(2)}, u32[]{:S(2)}) collective-permute-start(bf16[2,768,384]{1,2,0:T(8,128)(2,1)} %get-tuple-element.329), channel_id=1, source_target_pairs={{0,16},{16,32},{32,48},{48,64},{64,80},{80,96},{96,112},{112,128},... | collective-permute-start | bytes 3538952 | tf_op jit(solution)/shard_map/while/body/ppermute | solution.py:13
  159.5 9.1 %copy-start.3 = (pred[768,768]{0,1:T(8,128)(4,1)S(1)}, pred[768,768]{0,1:T(8,128)(4,1)}, u32[]{:S(2)}) copy-start(pred[768,768]{0,1:T(8,128)(4,1)} %copy.76) | copy-start | bytes 1769476 | tf_op jit(solution)/shard_map/while
  159.6 9.1 %copy-start.6 = (bf16[1,768,384]{1,2,0:T(8,128)(2,1)S(1)}, bf16[1,768,384]{1,2,0:T(8,128)(2,1)}, u32[]{:S(2)}) copy-start(bf16[1,768,384]{1,2,0:T(8,128)(2,1)} %get-tuple-element.347) | copy-start | bytes 1769476 | tf_op jit(solution)/shard_map/while
  174.2 1.6 copy-start.1
  175.7 0.7 copy-start.7
  176.1 2.5 %copy-start.2 = (f32[768,384]{0,1:T(8,128)}, f32[768,384]{0,1:T(8,128)S(1)}, u32[]{:S(2)}) copy-start(f32[768,384]{0,1:T(8,128)S(1)} %bitcast_add_fusion.3) | copy-start | bytes 3538948 | tf_op jit(solution)/shard_map/while
  176.5 2.1 %copy-start.8 = (f32[3,768]{1,0:T(4,128)}, f32[3,768]{1,0:T(4,128)S(1)}, u32[]{:S(2)}) copy-start(f32[3,768]{1,0:T(4,128)S(1)} %add_add_fusion.2) | copy-start | bytes 27652 | tf_op jit(solution)/shard_map/while
Sparse Core Ops, SparseCore 0:
  9.1 58.6 all-gather.1
where the time goes:
time: 201 us; the launch traced here: 198 us
  waiting for transfers between devices  65.7 us (33%)
  matrix products  41.3 us (21%)
  blocking collectives  24.9 us (12%)
  local copies, waits for them, and re-layouts  24 us (12%)
  starting transfers between devices  17 us (8%)
  between operations  14.7 us (7%)
  other arithmetic  10.2 us (5%)
    all_gather x1, waiting for transfers between devices, shards(): piece = lax.all_gather(hidden, 'head', axis=0, tiled=True)  38.1 us
    ppermute x6, waiting for transfers between devices, shifted(): return lax.ppermute(block, axis, route)  26.9 us
    ppermute x6, starting transfers between devices, shifted(): return lax.ppermute(block, axis, route)  17 us
    dot_general x3, matrix products, shards(): jnp.dot(piece, qkv_weight[j], preferred_element_type=jnp.float32)  15.3 us
    pmax x1, blocking collectives, shards(): farthest = lax.pmax(jnp.stack([ahead, behind]), 'blk')  14.7 us
    dot_general x7, matrix products, tile_terms(): jnp.einsum('qhd,khd->hqk', query_h, keys_h, preferred_element_type=jnp.fl...  14 us
    dot_general x7, matrix products, tile_terms(): jnp.einsum('hqk,khd->qhd', weights.astype(jnp.bfloat16), values_h, prefer...  11.9 us
    broadcast_in_dim x14, local copies, waits for them, and re-layouts, tile_terms(): jnp.where(mask[None, :, None, :], jnp.exp(score), jnp.float32(0.0))  10.4 us
  transfers between devices with their start and end apart: 7, of which 4 were waited for; matrix products, arithmetic and copies ran while one was open for 14% of the time, Pallas kernels for 0%

commit v1 on v0

v1 whole, which is shorter than its diff:
```python
import functools

import jax
import jax.numpy as jnp
from jax import lax
from jax.experimental import pallas as pl
from jax.experimental.pallas import tpu as pltpu
from jax.sharding import PartitionSpec as P

HD = 128
TILE = 384
MESH = pl.DeviceIdType.MESH


def kernel(
    sizes,
    hidden, weight, bias, gains, lists, counts,
    out, q_out, kv_out, flag_out,
    hid, wv, qb, kv, acc, ob, flags, mask,
    own_sem, w_sem, hs_sem, hr_sem, ks_sem, kr_sem, os_sem, or_sem, fs_sem, fr_sem, x_sem,
):
    n_blk, n_dp, heads, slots, n_tiles = sizes
    chunk = hid.shape[1]
    half = chunk // 2
    width = heads * HD
    b = lax.axis_index("blk")
    h = lax.axis_index("head")
    d = lax.axis_index("dp")
    c = lax.rem(b, 2)
    z = lax.div(b, 2)
    n_z = n_blk // 2
    right = lax.rem(h + 1, 4)
    opp = lax.rem(h + 2, 4)
    left = lax.rem(h + 3, 4)
    hb = lax.rem(h, 2)
    t0 = lax.div(h, 2)
    mate = h + 1 - 2 * hb
    other = lax.rem(h + 3 + 2 * hb, 4)
    partner = b + 1 - 2 * c
    up = lax.rem(b + 2, n_blk)
    down = lax.rem(b + n_blk - 2, n_blk)
    dps = [lax.rem(d + i, n_dp) for i in range(1, n_dp)]

    own_in = pltpu.make_async_copy(hidden, hid.at[h], own_sem)
    own_in.start()
    w_in = [pltpu.make_async_copy(weight.at[j], wv.at[j], w_sem.at[j]) for j in (1, 2, 0)]
    for copy in w_in:
        copy.start()

    barrier = pltpu.get_barrier_semaphore()
    for p in (right, opp, left):
        pl.semaphore_signal(barrier, inc=1, device_id={"head": p}, device_id_type=MESH)
    for p in (partner, up, down):
        pl.semaphore_signal(barrier, inc=1, device_id={"blk": p}, device_id_type=MESH)
    for p in dps:
        pl.semaphore_signal(barrier, inc=1, device_id={"dp": p}, device_id_type=MESH)
    pl.semaphore_wait(barrier, 6 + len(dps))

    def hid_send(src, slot, start, to, k):
        return pltpu.make_async_remote_copy(
            src_ref=src,
            dst_ref=hid.at[slot, pl.ds(start, half)],
            send_sem=hs_sem.at[k],
            recv_sem=hr_sem.at[k],
            device_id={"head": to},
            device_id_type=MESH,
        )

    top = hidden.at[pl.ds(0, half)]
    bottom = hidden.at[pl.ds(half, half)]
    hops = [
        hid_send(top, h, 0, right, 0),
        hid_send(bottom, h, half, left, 3),
        hid_send(bottom, h, half, right, 1),
        hid_send(top, h, 0, left, 4),
        hid_send(hid.at[left, pl.ds(0, half)], left, 0, right, 2),
        hid_send(hid.at[right, pl.ds(half, half)], right, half, left, 5),
    ]
    for copy in hops[:4]:
        copy.start()

    def hid_wait(slot, start, k):
        part = hid.at[slot, pl.ds(start, half)]
        pltpu.make_async_copy(part, part, hr_sem.at[k]).wait()

    def rows_of(core, part):
        return pl.ds(pl.multiple_of(core * TILE + part * chunk, chunk), chunk)

    def kv_copy(src_f, dst_f, kt, part, to, kind, stage):
        rows = rows_of(c, part)
        return pltpu.make_async_remote_copy(
            src_ref=kv.at[src_f, kt, rows],
            dst_ref=kv.at[dst_f, kt, rows],
            send_sem=ks_sem.at[kind, stage],
            recv_sem=kr_sem.at[kind, stage],
            device_id={"blk": to},
            device_id_type=MESH,
        )

    def kv_wait(f, kt, core, part, kind, stage):
        ref = kv.at[f, kt, rows_of(core, part)]
        pltpu.make_async_copy(ref, ref, kr_sem.at[kind, stage]).wait()

    part_of = [hb, 1 - hb, 1 - hb, hb]
    slot_of = [h, mate, other, opp]

    def project(stage, first):
        kt, part, slot = stage // 2, part_of[stage], slot_of[stage]
        x = hid[slot]
        for n, j in enumerate((1, 2, 0)):
            if first:
                w_in[n].wait()
            made = jnp.dot(x, wv[j], preferred_element_type=jnp.float32)
            made = made + bias[pl.ds(j, 1), :].astype(jnp.float32)
            for g in range(heads):
                cols = slice(g * HD, (g + 1) * HD)
                piece = made[:, cols]
                if j < 2:
                    mean_sq = jnp.mean(piece * piece, axis=-1, keepdims=True)
                    piece = piece * lax.rsqrt(mean_sq + 1e-06) * gains[pl.ds(j, 1), :]
                piece = piece.astype(jnp.bfloat16)
                if j == 0:
                    rows = pl.ds(pl.multiple_of(part * chunk, chunk), chunk)
                    qb[kt, rows, cols] = piece
                else:
                    off = (j - 1) * width + g * HD
                    kv[1, kt, rows_of(c, part), off : off + HD] = piece
        kv_copy(1, 2, kt, part, down, 2, stage).start()
        kv_copy(1, 0, kt, part, up, 1, stage).start()
        kv_copy(1, 1, kt, part, partner, 0, stage).start()

    def relay(stage):
        kt, part = stage // 2, part_of[stage]
        kv_wait(0, kt, c, part, 1, stage)
        kv_copy(0, 0, kt, part, partner, 3, stage).start()
        kv_wait(2, kt, c, part, 2, stage)
        kv_copy(2, 2, kt, part, partner, 4, stage).start()

    def near(stage):
        kv_wait(1, stage // 2, 1 - c, part_of[stage], 0, stage)

    def far(stage):
        kv_wait(0, stage // 2, 1 - c, part_of[stage], 3, stage)
        kv_wait(2, stage // 2, 1 - c, part_of[stage], 4, stage)

    own_in.wait()
    project(0, True)

    def check_row(t, bad):
        n = counts[t]
        for s in range(slots):
            gap = lax.rem(lists[t, s] // 4 - t // 4 + n_z, n_z)
            far_one = jnp.where((gap > 1) & (gap < n_z - 1) & (s < n), 1, 0)
            bad = jnp.maximum(bad, far_one)
        return bad

    bad = lax.fori_loop(0, n_tiles, check_row, jnp.int32(0))
    flags[d] = jnp.full(flags.shape[1:], bad, jnp.int32)

    def mask_entry(i, carry):
        q = i // 12
        f = lax.rem(i // 4, 3)
        kt = lax.rem(i // 2, 2)
        core = lax.rem(i, 2)
        row = 2 * b + lax.rem(t0 + q, 2)
        tile = 4 * lax.rem(z + f + n_z - 1, n_z) + 2 * core + lax.rem(t0 + kt, 2)
        n = counts[row]
        hit = jnp.int32(0)
        for s in range(slots):
            hit = jnp.maximum(hit, jnp.where((lists[row, s] == tile) & (s < n), 1, 0))
        mask[i] = hit.astype(jnp.float32)
        return carry

    lax.fori_loop(0, 24, mask_entry, 0)

    def flag_send(i, to):
        return pltpu.make_async_remote_copy(
            src_ref=flags.at[d],
            dst_ref=flags.at[d],
            send_sem=fs_sem.at[i],
            recv_sem=fr_sem.at[i],
            device_id={"dp": to},
            device_id_type=MESH,
        )

    flag_sends = [flag_send(i, p) for i, p in enumerate(dps)]
    for copy in flag_sends:
        copy.start()

    acc[...] = jnp.zeros_like(acc)

    hid_wait(left, 0, 0)
    hops[4].start()
    hid_wait(right, half, 3)
    hops[5].start()
    relay(0)
    for i, p in enumerate(dps):
        src = lax.rem(d + n_dp - 1 - i, n_dp)
        ref = flags.at[src]
        pltpu.make_async_copy(ref, ref, fr_sem.at[i]).wait()
    flag_out[...] = jnp.max(flags[...], axis=0)
    hid_wait(left, half, 1)
    hid_wait(right, 0, 4)
    project(1, False)
    project(2, False)
    near(0)
    near(1)

    def attend(q, f, kt):
        base = q * 12 + f * 4 + kt * 2
        live = jnp.concatenate(
            [
                jnp.full((TILE, HD), mask[base], jnp.float32),
                jnp.full((TILE, HD), mask[base + 1], jnp.float32),
            ],
            axis=0,
        ).astype(jnp.bfloat16)
        for g in range(heads):
            qh = qb[q, :, g * HD : (g + 1) * HD]
            kh = kv[f, kt, :, g * HD : (g + 1) * HD]
            vh = kv[f, kt, :, width + g * HD : width + (g + 1) * HD]
            score = lax.dot_general(
                qh, kh, (((1,), (1,)), ((), ())), preferred_element_type=jnp.float32
            )
            w = jnp.exp(score * HD ** (-0.5)).astype(jnp.bfloat16)
            ext = jnp.concatenate([vh * live, live], axis=1)
            acc[q, g] += jnp.dot(w, ext, preferred_element_type=jnp.float32)

    def finish(q):
        for g in range(heads):
            full = acc[q, g]
            ob[q, :, g * HD : (g + 1) * HD] = (full[:, :HD] / full[:, HD:]).astype(jnp.bfloat16)

    cols = pl.ds(pl.multiple_of(h * width, width), width)

    def out_send(q, part, to, k):
        return pltpu.make_async_remote_copy(
            src_ref=ob.at[q, pl.ds(pl.multiple_of(part * chunk, chunk), chunk)],
            dst_ref=out.at[:, cols],
            send_sem=os_sem.at[k],
            recv_sem=or_sem.at[k],
            device_id={"head": to},
            device_id_type=MESH,
        )

    out_sends = [
        out_send(1, hb, opp, 0),
        out_send(1, 1 - hb, other, 1),
        out_send(0, 1 - hb, mate, 2),
    ]
    own_out = pltpu.make_async_copy(
        ob.at[0, pl.ds(pl.multiple_of(hb * chunk, chunk), chunk)], out.at[:, cols], own_sem
    )

    def first_half(i, carry):
        j = lax.rem(i, 3)

        @pl.when(i == 1)
        def _():
            relay(1)
            far(0)
            far(1)

        @pl.when(i == 3)
        def _():
            hid_wait(opp, 0, 2)
            hid_wait(opp, half, 5)
            project(3, False)
            relay(2)

        attend(lax.div(i, 3), lax.rem(2 * j + 1, 3), 0)
        return carry

    lax.fori_loop(0, 6, first_half, 0)
    near(2)
    near(3)
    keep = [
        pltpu.make_async_copy(qb, q_out, x_sem.at[0]),
        pltpu.make_async_copy(kv.at[1, :, pl.ds(pl.multiple_of(c * TILE, TILE), TILE)], kv_out, x_sem.at[1]),
    ]
    for copy in keep:
        copy.start()

    def second_half(i, carry):
        g = lax.div(i, 2)
        new = lax.div(g + 1, 2)

        @pl.when(i == 2)
        def _():
            relay(3)
            far(2)
            far(3)

        attend(
            (1 - new) * (1 - i) + new * (2 - g),
            1 - new + new * 2 * lax.rem(i, 2),
            1,
        )

        @pl.when(i == 3)
        def _():
            finish(1)
            out_sends[0].start()
            out_sends[1].start()

        return carry

    lax.fori_loop(0, 6, second_half, 0)
    finish(0)
    out_sends[2].start()
    own_out.start()

    for copy in hops:
        copy.wait_send()
    for stage in range(4):
        kt, part = stage // 2, part_of[stage]
        kv_copy(1, 1, kt, part, partner, 0, stage).wait_send()
        kv_copy(1, 0, kt, part, up, 1, stage).wait_send()
        kv_copy(1, 2, kt, part, down, 2, stage).wait_send()
        kv_copy(0, 0, kt, part, partner, 3, stage).wait_send()
        kv_copy(2, 2, kt, part, partner, 4, stage).wait_send()
    for copy in flag_sends:
        copy.wait_send()
    for copy in keep:
        copy.wait()
    own_out.wait()
    for copy in out_sends:
        copy.wait_send()
    for k, src in enumerate((opp, other, mate)):
        ref = out.at[:, pl.ds(pl.multiple_of(src * width, width), width)]
        pltpu.make_async_copy(ref, ref, or_sem.at[k]).wait()


def window_attention(hidden, weight, bias, gains, lists, counts):
    n_blk = lax.axis_size("blk")
    n_dp = lax.axis_size("dp")
    chunk, depth = hidden.shape
    width = weight.shape[2]
    heads = width // HD
    n_tiles, slots = lists.shape
    sizes = (n_blk, n_dp, heads, slots, n_tiles)
    hbm = pl.BlockSpec(memory_space=pl.ANY)
    vmem = pl.BlockSpec(memory_space=pltpu.VMEM)
    smem = pl.BlockSpec(memory_space=pltpu.SMEM)
    dma = pltpu.SemaphoreType.DMA
    return pl.pallas_call(
        functools.partial(kernel, sizes),
        out_shape=(
            jax.ShapeDtypeStruct((chunk, 4 * width), jnp.bfloat16),
            jax.ShapeDtypeStruct((2, TILE, width), jnp.bfloat16),
            jax.ShapeDtypeStruct((2, TILE, 2 * width), jnp.bfloat16),
            jax.ShapeDtypeStruct((8, 128), jnp.int32),
        ),
        in_specs=[hbm, hbm, vmem, vmem, smem, smem],
        out_specs=(hbm, hbm, hbm, vmem),
        scratch_shapes=[
            pltpu.VMEM((4, chunk, depth), jnp.bfloat16),
            pltpu.VMEM((3, depth, width), jnp.bfloat16),
            pltpu.VMEM((2, TILE, width), jnp.bfloat16),
            pltpu.VMEM((3, 2, 2 * TILE, 2 * width), jnp.bfloat16),
            pltpu.VMEM((2, heads, TILE, 2 * HD), jnp.float32),
            pltpu.VMEM((2, TILE, width), jnp.bfloat16),
            pltpu.VMEM((n_dp, 8, 128), jnp.int32),
            pltpu.SMEM((24,), jnp.float32),
            dma,
            dma((3,)),
            dma((6,)),
            dma((6,)),
            dma((5, 4)),
            dma((5, 4)),
            dma((3,)),
            dma((3,)),
            dma((n_dp - 1,)),
            dma((n_dp - 1,)),
            dma((2,)),
        ],
        compiler_params=pltpu.CompilerParams(
            collective_id=0, has_side_effects=True, vmem_limit_bytes=60 * 1024 * 1024
        ),
    )(hidden, weight, bias, gains, lists, counts)


def any_lists(query, key_value, tile_lists, tile_counts):
    n_blk = lax.axis_size("blk")
    place = lax.axis_index("blk")
    t0 = lax.axis_index("head") // 2
    width = query.shape[2]
    heads = width // HD
    rows = 2 * TILE

    def in_order(tiles):
        return jnp.where(t0 == 0, tiles, tiles[::-1]).reshape(rows, -1)

    query = in_order(query).reshape(rows, heads, HD)
    current = in_order(key_value)
    lists = lax.dynamic_slice_in_dim(tile_lists, place * 2, 2, 0)
    counts = lax.dynamic_slice_in_dim(tile_counts, place * 2, 2, 0)
    live = jnp.arange(lists.shape[1], dtype=jnp.int32)[None, :] < counts[:, None]
    route = [(i, (i - 1) % n_blk) for i in range(n_blk)]

    def turn(step, carry):
        total, numer, block = carry
        key_tile = 2 * ((place + step) % n_blk) + jnp.arange(rows, dtype=jnp.int32) // TILE
        hits = (lists[:, :, None] == key_tile[None, None, :]) & live[:, :, None]
        mask = jnp.repeat(jnp.any(hits, axis=1), TILE, axis=0)
        keys = block[:, :width].reshape(rows, heads, HD)
        values = block[:, width:].reshape(rows, heads, HD)
        score = jnp.einsum("qhd,khd->hqk", query, keys, preferred_element_type=jnp.float32)
        w = jnp.where(mask[None], jnp.exp(score * HD ** (-0.5)), jnp.float32(0.0))
        total = total + jnp.sum(w, axis=-1)
        numer = numer + jnp.einsum(
            "hqk,khd->hqd", w.astype(jnp.bfloat16), values, preferred_element_type=jnp.float32
        )
        return (total, numer, lax.ppermute(block, "blk", route))

    total, numer, current = lax.fori_loop(
        0,
        n_blk,
        turn,
        (
            jnp.zeros((heads, rows), jnp.float32),
            jnp.zeros((heads, rows, HD), jnp.float32),
            current,
        ),
    )
    attended = (numer / total[:, :, None]).transpose(1, 0, 2).reshape(rows, width)
    return lax.all_to_all(
        attended.astype(jnp.bfloat16), "head", split_axis=0, concat_axis=1, tiled=True
    )


def shards(hidden, qkv_weight, qkv_bias, norm_gains, tile_lists, tile_counts):
    out, query, key_value, flag = window_attention(
        hidden, qkv_weight, qkv_bias, norm_gains, tile_lists, tile_counts
    )
    return lax.cond(
        flag[0, 0] > 0,
        lambda: any_lists(query, key_value, tile_lists, tile_counts),
        lambda: out,
    )


def solution(mesh):
    return jax.shard_map(
        shards,
        mesh=mesh,
        in_specs=(
            P(("dp", "blk", "head"), None),
            P(None, None, "head"),
            P(None, "head"),
            P(),
            P("dp", None),
            P("dp"),
        ),
        out_specs=P(("dp", "blk", "head"), None),
        check_vma=False,
    )
```

time: 201 us -> 80.5 us (0.40); the launches traced: 198 us -> 80.3 us
  Pallas kernels: 0 us -> 76.2 us
  waiting for transfers between devices: 65.7 us -> 0 us
  matrix products: 41.3 us -> 0 us
  blocking collectives: 24.9 us -> 0 us
  local copies, waits for them, and re-layouts: 24 us -> 3.4 us
  starting transfers between devices: 17 us -> 0 us
  between operations: 14.7 us -> 0.69 us
  other arithmetic: 10.2 us -> 0 us
    pallas_call x0 -> x1, Pallas kernels: none -> 76.2 us  [window_attention(): pl.pallas_call(functools.partial(kernel, sizes), out_shape=(jax.ShapeDtyp...]
    dot_general x17 -> x0, matrix products: 41.3 us -> none  [the longest x3 15.3 us: shards(): jnp.dot(piece, qkv_weight[j], preferred_element_type=jnp.float32)]
    all_gather x1 -> x0, waiting for transfers between devices: 38.1 us -> none  [shards(): piece = lax.all_gather(hidden, 'head', axis=0, tiled=True)]
    ppermute x6 -> x0, waiting for transfers between devices: 26.9 us -> none  [shifted(): return lax.ppermute(block, axis, route)]
    ppermute x6 -> x0, starting transfers between devices: 17 us -> none  [shifted(): return lax.ppermute(block, axis, route)]
    pmax x1 -> x0, blocking collectives: 14.7 us -> none  [shards(): farthest = lax.pmax(jnp.stack([ahead, behind]), 'blk')]
    broadcast_in_dim x14 -> x0, local copies, waits for them, and re-layouts: 10.4 us -> none  [tile_terms(): jnp.where(mask[None, :, None, :], jnp.exp(score), jnp.float32(0.0))]
    all_to_all x1 -> x0, blocking collectives: 10.2 us -> none  [shards(): lax.all_to_all(attended, 'head', split_axis=0, concat_axis=1, tiled=True)]
  transfers between devices with their start and end apart: 7 -> 0, of which waited for: 4 -> 0; matrix products, arithmetic and copies ran while one was open for 14% -> 0% of each run, Pallas kernels for 0% -> 0%
where the time goes in v1:
time: 80.5 us; the launch traced here: 80.3 us
  Pallas kernels  76.2 us (95%)
  local copies, waits for them, and re-layouts  3.4 us (4%)
    pallas_call x1, Pallas kernels, window_attention(): pl.pallas_call(functools.partial(kernel, sizes), out_shape=(jax.ShapeDtyp...  76.2 us
    unnamed x6, local copies, waits for them, and re-layouts  2.2 us

profile of v1, /device:TPU:1, one launch (start us, length us, event | category | flops | bytes accessed | tf_op | source)
XLA Modules:
  0.0 80.3 jit_solution(8637046077273728527)
XLA Ops:
  0.0 1.4 %copy.40.lists = s32[32,12]{1,0:T(8,128)} copy(s32[32,12]{0,1:T(8,128)} %param.14) | data formatting | bytes 3072 | tf_op args[4]
  1.4 0.0 copy-start.3
  1.4 0.0 copy-start.4
  1.4 76.2 %shard_map.66 = (bf16[192,1536]{1,0:T(8,128)(2,1)S(1)}, bf16[2,384,384]{2,1,0:T(8,128)(2,1)S(1)}, bf16[2,384,768]{2,1,0:T(8,128)(2,1)S(1)}, s32[8,128]{1,0:T(8,128)}) custom-call(bf16[192,3072]{1,0:T(8,128)(2,1)} %hidden.1, bf16[3,3072,384]{2,1,0:T(8,128)(2,1)} %weight.1, bf16[3,384]{1,0:T(4,128)(2,1)} %bias.1, f32[2,128]{1,0:T(2,128)} %gains.1, ...), custom_call_target="tpu_custom_call" | custom-call | tf_op jit(solution)/shard_map/pallas_call | solution.py:346
  77.6 1.2 %slice.23 = s32[1,1]{1,0:T(1,128)} slice(s32[8,128]{1,0:T(8,128)} %get-tuple-element.227), slice={[0:1], [0:1]} | slice | bytes 8 | tf_op jit(solution)/shard_map/slice | solution.py:437
  79.4 0.0 copy-done.3
  79.5 0.0 copy-done.4
  79.5 0.8 %copy.66 = bf16[192,1536]{1,0:T(8,128)(2,1)} copy(bf16[192,1536]{1,0:T(8,128)(2,1)S(1)} %get-tuple-element.231) | data formatting | bytes 1179648
  (1 shorter events, 0.0 us)
Async XLA Ops:
  1.4 78.1 %copy-start.3 = (s32[32,12]{0,1:T(8,128)S(1)}, s32[32,12]{0,1:T(8,128)}, u32[]{:S(2)}) copy-start(s32[32,12]{0,1:T(8,128)} %param.14) | copy-start | bytes 4612
  1.4 78.1 %copy-start.4 = (s32[32]{0:T(128)S(1)}, s32[32]{0:T(128)}, u32[]{:S(2)}) copy-start(s32[32]{0:T(128)} %counts.1) | copy-start | bytes 388

commit v2 on v1

v2 whole, which is shorter than its diff:
```python
import functools

import jax
import jax.numpy as jnp
from jax import lax
from jax.experimental import pallas as pl
from jax.experimental.pallas import tpu as pltpu
from jax.sharding import PartitionSpec as P

HD = 128
TILE = 384
MESH = pl.DeviceIdType.MESH


def kernel(
    sizes,
    hidden, weight, bias, gains, lists, counts,
    out, q_out, kv_out, flag_out,
    hid, wv, qb, kv, acc, ob, passing, flags, mask,
    own_sem, w_sem, hs_sem, hr_sem, ks_sem, kr_sem, os_sem, or_sem, fs_sem, fr_sem, x_sem,
):
    n_blk, n_dp, heads, slots, n_tiles = sizes
    chunk = hid.shape[1]
    half = chunk // 2
    quarter = chunk // 4
    width = heads * HD
    b = lax.axis_index("blk")
    h = lax.axis_index("head")
    d = lax.axis_index("dp")
    c = lax.rem(b, 2)
    z = lax.div(b, 2)
    n_z = n_blk // 2
    right = lax.rem(h + 1, 4)
    opp = lax.rem(h + 2, 4)
    left = lax.rem(h + 3, 4)
    hb = lax.rem(h, 2)
    t0 = lax.div(h, 2)
    mate = h + 1 - 2 * hb
    other = lax.rem(h + 3 + 2 * hb, 4)
    partner = b + 1 - 2 * c
    up = lax.rem(b + 2, n_blk)
    down = lax.rem(b + n_blk - 2, n_blk)
    dps = [lax.rem(d + i, n_dp) for i in range(1, n_dp)]

    own_in = pltpu.make_async_copy(hidden, hid.at[0], own_sem)
    own_in.start()
    w_in = [pltpu.make_async_copy(weight.at[j], wv.at[j], w_sem.at[j]) for j in (1, 2, 0)]
    for copy in w_in:
        copy.start()

    barrier = pltpu.get_barrier_semaphore()
    for p in (right, opp, left):
        pl.semaphore_signal(barrier, inc=1, device_id={"head": p}, device_id_type=MESH)
    for p in (partner, up, down):
        pl.semaphore_signal(barrier, inc=1, device_id={"blk": p}, device_id_type=MESH)
    for p in dps:
        pl.semaphore_signal(barrier, inc=1, device_id={"dp": p}, device_id_type=MESH)
    pl.semaphore_wait(barrier, 6 + len(dps))

    def hid_send(src, slot, start, rows, to, k):
        return pltpu.make_async_remote_copy(
            src_ref=src.at[pl.ds(start, rows)],
            dst_ref=hid.at[slot, pl.ds(start, rows)],
            send_sem=hs_sem.at[k],
            recv_sem=hr_sem.at[k],
            device_id={"head": to},
            device_id_type=MESH,
        )

    hops = [
        hid_send(hidden, 1, 0, half, right, 0),
        hid_send(hidden, 2, half, half, left, 4),
        hid_send(hidden, 1, half, half, right, 1),
        hid_send(hidden, 2, 0, half, left, 5),
        hid_send(hid.at[1], 3, 0, quarter, right, 2),
        hid_send(hid.at[2], 3, 3 * quarter, quarter, left, 6),
        hid_send(hid.at[1], 3, quarter, quarter, right, 3),
        hid_send(hid.at[2], 3, 2 * quarter, quarter, left, 7),
    ]
    for copy in hops[:4]:
        copy.start()

    def hid_wait(slot, start, rows, k):
        part = hid.at[slot, pl.ds(start, rows)]
        pltpu.make_async_copy(part, part, hr_sem.at[k]).wait()

    mate_left = hb
    left_block = 2 - mate_left
    right_block = 1 + mate_left
    batches = [
        (0, chunk, [(0, 0, chunk, 0, 0)]),
        (2 * chunk, chunk, [(1, 0, half, left_block, 0), (2, half, half, right_block, half)]),
        (4 * chunk, chunk, [(1, half, half, left_block, half), (2, 0, half, right_block, 0)]),
        (6 * chunk, half, [(3, 0, quarter, 3, 0), (3, 3 * quarter, quarter, 3, 3 * quarter)]),
        (7 * chunk, half, [(3, quarter, half, 3, quarter)]),
    ]

    def key_rows(n, core):
        first, rows, _ = batches[n]
        return pl.ds(pl.multiple_of(first + core * rows, rows), rows)

    def kv_copy(src_f, dst_f, n, to, kind):
        rows = key_rows(n, c)
        return pltpu.make_async_remote_copy(
            src_ref=kv.at[src_f, rows],
            dst_ref=kv.at[dst_f, rows],
            send_sem=ks_sem.at[kind, n],
            recv_sem=kr_sem.at[kind, n],
            device_id={"blk": to},
            device_id_type=MESH,
        )

    def kv_wait(f, n, core, kind):
        ref = kv.at[f, key_rows(n, core)]
        pltpu.make_async_copy(ref, ref, kr_sem.at[kind, n]).wait()

    def project(n):
        _, _, pieces = batches[n]
        parts = [hid[slot, start : start + rows] for slot, start, rows, _, _ in pieces]
        x = parts[0] if len(parts) == 1 else jnp.concatenate(parts, axis=0)
        for order, j in enumerate((1, 2, 0)):
            if n == 0:
                w_in[order].wait()
            made = jnp.dot(x, wv[j], preferred_element_type=jnp.float32)
            made = made + bias[pl.ds(j, 1), :].astype(jnp.float32)
            for g in range(heads):
                cols = slice(g * HD, (g + 1) * HD)
                piece = made[:, cols]
                if j < 2:
                    mean_sq = jnp.mean(piece * piece, axis=-1, keepdims=True)
                    piece = piece * lax.rsqrt(mean_sq + 1e-06) * gains[pl.ds(j, 1), :]
                piece = piece.astype(jnp.bfloat16)
                if j == 0:
                    at = 0
                    for _, _, rows, block, start in pieces:
                        qb[block, start : start + rows, cols] = piece[at : at + rows]
                        at += rows
                else:
                    off = (j - 1) * width + g * HD
                    kv[1, key_rows(n, c), off : off + HD] = piece
            if j == 2:
                kv_copy(1, 2, n, down, 2).start()
                kv_copy(1, 0, n, up, 1).start()
                kv_copy(1, 1, n, partner, 0).start()

    def relay(n):
        kv_wait(0, n, c, 1)
        kv_copy(0, 0, n, partner, 3).start()
        kv_wait(2, n, c, 2)
        kv_copy(2, 2, n, partner, 4).start()

    def near(n):
        kv_wait(1, n, 1 - c, 0)

    def far(n):
        kv_wait(0, n, 1 - c, 3)
        kv_wait(2, n, 1 - c, 4)

    own_in.wait()
    project(0)

    def check_row(t, bad):
        n = counts[t]
        for s in range(slots):
            gap = lax.rem(lists[s, t] // 4 - t // 4 + n_z, n_z)
            far_one = jnp.where((gap > 1) & (gap < n_z - 1) & (s < n), 1, 0)
            bad = jnp.maximum(bad, far_one)
        return bad

    bad = lax.fori_loop(0, n_tiles, check_row, jnp.int32(0))
    flags[d] = jnp.full(flags.shape[1:], bad, jnp.int32)

    def mask_entry(i, carry):
        q = i // 12
        f = lax.rem(i // 4, 3)
        kt = lax.rem(i // 2, 2)
        core = lax.rem(i, 2)
        row = 2 * b + lax.rem(t0 + q, 2)
        tile = 4 * lax.rem(z + f + n_z - 1, n_z) + 2 * core + lax.rem(t0 + kt, 2)
        n = counts[row]
        hit = jnp.int32(0)
        for s in range(slots):
            hit = jnp.maximum(hit, jnp.where((lists[s, row] == tile) & (s < n), 1, 0))
        mask[i] = hit.astype(jnp.float32)
        return carry

    lax.fori_loop(0, 24, mask_entry, 0)

    def flag_send(i, to):
        return pltpu.make_async_remote_copy(
            src_ref=flags.at[d],
            dst_ref=flags.at[d],
            send_sem=fs_sem.at[i],
            recv_sem=fr_sem.at[i],
            device_id={"dp": to},
            device_id_type=MESH,
        )

    flag_sends = [flag_send(i, p) for i, p in enumerate(dps)]
    for copy in flag_sends:
        copy.start()

    acc[...] = jnp.zeros_like(acc)

    segments = {
        0: [(chunk, 0, 0), (chunk, 0, 1)],
        1: [(half, 1 - mate_left, 0), (half, mate_left, 0), (half, 1 - mate_left, 1), (half, mate_left, 1)],
        3: [(half, 1, 0), (half, 1, 1)],
    }
    segments[2] = segments[1]
    segments[4] = segments[3]

    def attend(block, tile, f, group):
        base = tile * 12 + f * 4
        live = jnp.concatenate(
            [
                jnp.full((rows, HD), mask[base + kt * 2 + core], jnp.float32)
                for n in group
                for rows, kt, core in segments[n]
            ],
            axis=0,
        ).astype(jnp.bfloat16)
        keys = slice(batches[group[0]][0], batches[group[0]][0] + live.shape[0])
        for g in range(heads):
            qh = qb[block, :, g * HD : (g + 1) * HD]
            kh = kv[f, keys, g * HD : (g + 1) * HD]
            vh = kv[f, keys, width + g * HD : width + (g + 1) * HD]
            score = lax.dot_general(
                qh, kh, (((1,), (1,)), ((), ())), preferred_element_type=jnp.float32
            )
            w = jnp.exp(score * HD ** (-0.5)).astype(jnp.bfloat16)
            ext = jnp.concatenate([vh * live, live], axis=1)
            acc[block, g] += jnp.dot(w, ext, preferred_element_type=jnp.float32)

    def finish(block):
        for g in range(heads):
            full = acc[block, g]
            ob[block, :, g * HD : (g + 1) * HD] = (full[:, :HD] / full[:, HD:]).astype(jnp.bfloat16)

    def columns(p):
        return pl.ds(pl.multiple_of(p * width, width), width)

    def out_send(src, dst, to, k):
        return pltpu.make_async_remote_copy(
            src_ref=src,
            dst_ref=dst,
            send_sem=os_sem.at[k],
            recv_sem=or_sem.at[k],
            device_id={"head": to},
            device_id_type=MESH,
        )

    upper, lower = pl.ds(0, half), pl.ds(half, half)
    out_sends = [
        out_send(ob.at[3, upper], passing.at[0], right, 0),
        out_send(ob.at[3, lower], passing.at[1], left, 1),
        out_send(ob.at[2], out.at[:, columns(h)], other, 2),
        out_send(ob.at[1], out.at[:, columns(h)], mate, 3),
        out_send(passing.at[0], out.at[upper, columns(left)], right, 4),
        out_send(passing.at[1], out.at[lower, columns(right)], left, 5),
    ]
    own_out = pltpu.make_async_copy(ob.at[0], out.at[:, columns(h)], own_sem)

    hid_wait(1, 0, half, 0)
    hops[4].start()
    hops[6].start()
    hid_wait(2, half, half, 4)
    hops[5].start()
    hops[7].start()
    relay(0)
    project(1)
    for i in range(n_dp - 1):
        src = lax.rem(d + n_dp - 1 - i, n_dp)
        ref = flags.at[src]
        pltpu.make_async_copy(ref, ref, fr_sem.at[i]).wait()
    flag_out[...] = jnp.max(flags[:, 0:1, 0:1], axis=0)
    near(0)
    near(1)

    def own_first(i, carry):
        @pl.when(i == 1)
        def _():
            relay(1)
            far(0)
            far(1)

        attend(0, 0, lax.rem(2 * i + 1, 3), (0, 1))
        return carry

    lax.fori_loop(0, 3, own_first, 0)
    hid_wait(1, half, half, 1)
    hid_wait(2, 0, half, 5)
    project(2)

    def neighbours_first(i, carry):
        block = 1 + lax.div(i, 3)
        attend(block, lax.div(block, 2), lax.rem(i, 3), (0, 1))
        return carry

    lax.fori_loop(0, 6, neighbours_first, 0)
    hid_wait(3, 0, quarter, 2)
    hid_wait(3, 3 * quarter, quarter, 6)
    project(3)
    relay(2)
    near(2)
    near(3)

    def own_second(i, carry):
        attend(i, lax.div(i, 2), 1, (2, 3))
        return carry

    lax.fori_loop(0, 3, own_second, 0)
    relay(3)
    hid_wait(3, quarter, quarter, 3)
    hid_wait(3, 2 * quarter, quarter, 7)
    project(4)

    def opposite_first(i, carry):
        attend(3, 1, i, (0, 1))
        return carry

    lax.fori_loop(0, 3, opposite_first, 0)
    keep = [pltpu.make_async_copy(qb, q_out, x_sem.at[5])]
    at = 0
    for n, (_, rows, _) in enumerate(batches):
        keep.append(pltpu.make_async_copy(kv.at[1, key_rows(n, c)], kv_out.at[pl.ds(at, rows)], x_sem.at[n]))
        at += rows
    for copy in keep:
        copy.start()
    far(2)
    far(3)

    def second(i, carry):
        new = lax.div(i + 8, 9)
        block = 3 - new * lax.div(i + 1 - 2 * new + (1 - new), 2)
        attend(block, lax.div(block, 2), (1 - new) + new * 2 * lax.rem(i, 2), (2, 3))
        return carry

    lax.fori_loop(0, 9, second, 0)
    relay(4)
    near(4)

    def last(i, carry):
        new = lax.div(i + 8, 12)

        @pl.when(i == 4)
        def _():
            far(4)

        block = (1 - new) * i + new * (5 - lax.div(i, 2))
        attend(block, lax.div(block, 2), (1 - new) + new * 2 * lax.rem(i, 2), (4,))

        @pl.when((i >= 4) & (lax.rem(i, 2) == 1))
        def _():
            finish(block)

        @pl.when(i == 5)
        def _():
            out_sends[0].start()
            out_sends[1].start()

        @pl.when(i == 7)
        def _():
            out_sends[2].start()

        @pl.when(i == 9)
        def _():
            out_sends[3].start()

        return carry

    lax.fori_loop(0, 12, last, 0)
    own_out.start()
    for k in range(2):
        ref = passing.at[k]
        pltpu.make_async_copy(ref, ref, or_sem.at[k]).wait()
        out_sends[4 + k].start()

    for copy in hops:
        copy.wait_send()
    for n in range(5):
        kv_copy(1, 1, n, partner, 0).wait_send()
        kv_copy(1, 0, n, up, 1).wait_send()
        kv_copy(1, 2, n, down, 2).wait_send()
        kv_copy(0, 0, n, partner, 3).wait_send()
        kv_copy(2, 2, n, partner, 4).wait_send()
    for copy in flag_sends:
        copy.wait_send()
    for copy in keep:
        copy.wait()
    own_out.wait()
    for copy in out_sends:
        copy.wait_send()
    for k, ref in (
        (2, out.at[:, columns(other)]),
        (3, out.at[:, columns(mate)]),
        (4, out.at[upper, columns(opp)]),
        (5, out.at[lower, columns(opp)]),
    ):
        pltpu.make_async_copy(ref, ref, or_sem.at[k]).wait()


def window_attention(hidden, weight, bias, gains, lists, counts):
    n_blk = lax.axis_size("blk")
    n_dp = lax.axis_size("dp")
    chunk, depth = hidden.shape
    width = weight.shape[2]
    heads = width // HD
    slots, n_tiles = lists.shape
    sizes = (n_blk, n_dp, heads, slots, n_tiles)
    hbm = pl.BlockSpec(memory_space=pl.ANY)
    vmem = pl.BlockSpec(memory_space=pltpu.VMEM)
    smem = pl.BlockSpec(memory_space=pltpu.SMEM)
    dma = pltpu.SemaphoreType.DMA
    return pl.pallas_call(
        functools.partial(kernel, sizes),
        out_shape=(
            jax.ShapeDtypeStruct((chunk, 4 * width), jnp.bfloat16),
            jax.ShapeDtypeStruct((4, chunk, width), jnp.bfloat16),
            jax.ShapeDtypeStruct((4 * chunk, 2 * width), jnp.bfloat16),
            jax.ShapeDtypeStruct((1, 1), jnp.int32),
        ),
        in_specs=[hbm, hbm, vmem, vmem, smem, smem],
        out_specs=(hbm, hbm, hbm, vmem),
        scratch_shapes=[
            pltpu.VMEM((4, chunk, depth), jnp.bfloat16),
            pltpu.VMEM((3, depth, width), jnp.bfloat16),
            pltpu.VMEM((4, chunk, width), jnp.bfloat16),
            pltpu.VMEM((3, 8 * chunk, 2 * width), jnp.bfloat16),
            pltpu.VMEM((4, heads, chunk, 2 * HD), jnp.float32),
            pltpu.VMEM((4, chunk, width), jnp.bfloat16),
            pltpu.VMEM((2, chunk // 2, width), jnp.bfloat16),
            pltpu.VMEM((n_dp, 8, 128), jnp.int32),
            pltpu.SMEM((24,), jnp.float32),
            dma,
            dma((3,)),
            dma((8,)),
            dma((8,)),
            dma((5, 5)),
            dma((5, 5)),
            dma((6,)),
            dma((6,)),
            dma((n_dp - 1,)),
            dma((n_dp - 1,)),
            dma((6,)),
        ],
        compiler_params=pltpu.CompilerParams(
            collective_id=0, has_side_effects=True, vmem_limit_bytes=60 * 1024 * 1024
        ),
    )(hidden, weight, bias, gains, lists, counts)


def any_lists(query, key_value, tile_lists, tile_counts):
    n_blk = lax.axis_size("blk")
    place = lax.axis_index("blk")
    h = lax.axis_index("head")
    chunk, width = query.shape[1:]
    heads = width // HD
    rows = 2 * TILE
    half, quarter = chunk // 2, chunk // 4

    def in_order(own, right, opposite, left):
        around = jnp.concatenate([own, right, opposite, left] * 2, axis=0)
        return lax.dynamic_slice_in_dim(around, lax.rem(4 - h, 4) * chunk, rows, 0)

    odd = lax.rem(h, 2) == 1
    right_q = jnp.where(odd, query[2], query[1])
    left_q = jnp.where(odd, query[1], query[2])
    query = in_order(query[0], right_q, query[3], left_q).reshape(rows, heads, HD)
    one, two, opp = (key_value[i * chunk : (i + 1) * chunk] for i in (1, 2, 3))
    current = in_order(
        key_value[:chunk],
        jnp.concatenate([two[half:], one[half:]], axis=0),
        jnp.concatenate([opp[:quarter], opp[half:], opp[quarter:half]], axis=0),
        jnp.concatenate([one[:half], two[:half]], axis=0),
    )
    lists = lax.dynamic_slice_in_dim(tile_lists, place * 2, 2, 0)
    counts = lax.dynamic_slice_in_dim(tile_counts, place * 2, 2, 0)
    live = jnp.arange(lists.shape[1], dtype=jnp.int32)[None, :] < counts[:, None]
    route = [(i, (i - 1) % n_blk) for i in range(n_blk)]

    def turn(step, carry):
        total, numer, block = carry
        key_tile = 2 * ((place + step) % n_blk) + jnp.arange(rows, dtype=jnp.int32) // TILE
        hits = (lists[:, :, None] == key_tile[None, None, :]) & live[:, :, None]
        mask = jnp.repeat(jnp.any(hits, axis=1), TILE, axis=0)
        keys = block[:, :width].reshape(rows, heads, HD)
        values = block[:, width:].reshape(rows, heads, HD)
        score = jnp.einsum("qhd,khd->hqk", query, keys, preferred_element_type=jnp.float32)
        w = jnp.where(mask[None], jnp.exp(score * HD ** (-0.5)), jnp.float32(0.0))
        total = total + jnp.sum(w, axis=-1)
        numer = numer + jnp.einsum(
            "hqk,khd->hqd", w.astype(jnp.bfloat16), values, preferred_element_type=jnp.float32
        )
        return (total, numer, lax.ppermute(block, "blk", route))

    total, numer, current = lax.fori_loop(
        0,
        n_blk,
        turn,
        (
            jnp.zeros((heads, rows), jnp.float32),
            jnp.zeros((heads, rows, HD), jnp.float32),
            current,
        ),
    )
    attended = (numer / total[:, :, None]).transpose(1, 0, 2).reshape(rows, width)
    return lax.all_to_all(
        attended.astype(jnp.bfloat16), "head", split_axis=0, concat_axis=1, tiled=True
    )


def shards(hidden, qkv_weight, qkv_bias, norm_gains, tile_lists, tile_counts):
    out, query, key_value, flag = window_attention(
        hidden, qkv_weight, qkv_bias, norm_gains, tile_lists.T, tile_counts
    )
    return lax.cond(
        flag[0, 0] > 0,
        lambda: any_lists(query, key_value, tile_lists, tile_counts),
        lambda: out,
    )


def solution(mesh):
    return jax.shard_map(
        shards,
        mesh=mesh,
        in_specs=(
            P(("dp", "blk", "head"), None),
            P(None, None, "head"),
            P(None, "head"),
            P(),
            P("dp", None),
            P("dp"),
        ),
        out_specs=P(("dp", "blk", "head"), None),
        check_vma=False,
    )
```

time: 80.5 us -> 77.3 us (0.960)
  local copies, waits for them, and re-layouts: 3.4 us -> 0.82 us
    unnamed x6 -> x5, local copies, waits for them, and re-layouts: 2.2 us -> 0.82 us
    slice x1 -> x0, local copies, waits for them, and re-layouts: 1.2 us -> none  [shards(): flag[0, 0] > 0]
where the time goes in v2:
time: 77.3 us; the launch traced here: 77 us
  Pallas kernels  75.6 us (98%)
  local copies, waits for them, and re-layouts  0.82 us (1%)
    pallas_call x1, Pallas kernels, window_attention(): pl.pallas_call(functools.partial(kernel, sizes), out_shape=(jax.ShapeDtyp...  75.6 us

profile of v2, /device:TPU:1, one launch (start us, length us, event | category | flops | bytes accessed | tf_op | source)
XLA Modules:
  0.0 77.0 jit_solution(1923808065901752551)
XLA Ops:
  0.0 0.0 copy-start.8
  0.0 0.0 copy-start.9
  0.0 75.6 %shard_map.66 = (bf16[192,1536]{1,0:T(8,128)(2,1)S(1)}, bf16[4,192,384]{2,1,0:T(8,128)(2,1)S(1)}, bf16[768,768]{1,0:T(8,128)(2,1)S(1)}, s32[1,1]{1,0:T(1,128)}) custom-call(bf16[192,3072]{1,0:T(8,128)(2,1)} %hidden.1, bf16[3,3072,384]{2,1,0:T(8,128)(2,1)} %weight.1, bf16[3,384]{1,0:T(4,128)(2,1)} %bias.1, f32[2,128]{1,0:T(2,128)} %gains.1, ...), custom_call_target="tpu_custom_call" | custom-call | tf_op jit(solution)/shard_map/pallas_call | solution.py:415
  76.1 0.0 copy-done.8
  76.1 0.0 copy-done.9
  76.2 0.8 %copy.61 = bf16[192,1536]{1,0:T(8,128)(2,1)} copy(bf16[192,1536]{1,0:T(8,128)(2,1)S(1)} %get-tuple-element.231) | data formatting | bytes 1179648
  (1 shorter events, 0.0 us)
Async XLA Ops:
  0.0 76.1 %copy-start.8 = (s32[32,12]{0,1:T(8,128)S(1)}, s32[32,12]{0,1:T(8,128)}, u32[]{:S(2)}) copy-start(s32[32,12]{0,1:T(8,128)} %param.14) | copy-start | bytes 4612
  0.0 76.1 %copy-start.9 = (s32[32]{0:T(128)S(1)}, s32[32]{0:T(128)}, u32[]{:S(2)}) copy-start(s32[32]{0:T(128)} %counts.1) | copy-start | bytes 388

commit v3 on v2

--- a/solution.py
+++ b/solution.py
@@ -22,7 +22,8 @@
     n_blk, n_dp, heads, slots, n_tiles = sizes
     chunk = hid.shape[1]
     half = chunk // 2
-    quarter = chunk // 4
+    part = chunk // 3
+    rest = half - part
     width = heads * HD
     b = lax.axis_index("blk")
     h = lax.axis_index("head")
@@ -72,17 +73,17 @@
         hid_send(hidden, 2, half, half, left, 4),
         hid_send(hidden, 1, half, half, right, 1),
         hid_send(hidden, 2, 0, half, left, 5),
-        hid_send(hid.at[1], 3, 0, quarter, right, 2),
-        hid_send(hid.at[2], 3, 3 * quarter, quarter, left, 6),
-        hid_send(hid.at[1], 3, quarter, quarter, right, 3),
-        hid_send(hid.at[2], 3, 2 * quarter, quarter, left, 7),
+        hid_send(hid.at[1], 3, 0, part, right, 2),
+        hid_send(hid.at[2], 3, chunk - part, part, left, 6),
+        hid_send(hid.at[1], 3, part, rest, right, 3),
+        hid_send(hid.at[2], 3, half, rest, left, 7),
     ]
     for copy in hops[:4]:
         copy.start()
 
     def hid_wait(slot, start, rows, k):
-        part = hid.at[slot, pl.ds(start, rows)]
-        pltpu.make_async_copy(part, part, hr_sem.at[k]).wait()
+        ref = hid.at[slot, pl.ds(start, rows)]
+        pltpu.make_async_copy(ref, ref, hr_sem.at[k]).wait()
 
     mate_left = hb
     left_block = 2 - mate_left
@@ -91,8 +92,8 @@
         (0, chunk, [(0, 0, chunk, 0, 0)]),
         (2 * chunk, chunk, [(1, 0, half, left_block, 0), (2, half, half, right_block, half)]),
         (4 * chunk, chunk, [(1, half, half, left_block, half), (2, 0, half, right_block, 0)]),
-        (6 * chunk, half, [(3, 0, quarter, 3, 0), (3, 3 * quarter, quarter, 3, 3 * quarter)]),
-        (7 * chunk, half, [(3, quarter, half, 3, quarter)]),
+        (6 * chunk, 2 * part, [(3, 0, part, 3, 0), (3, chunk - part, part, 3, chunk - part)]),
+        (6 * chunk + 4 * part, 2 * rest, [(3, part, 2 * rest, 3, part)]),
     ]
 
     def key_rows(n, core):
@@ -118,30 +119,37 @@
         _, _, pieces = batches[n]
         parts = [hid[slot, start : start + rows] for slot, start, rows, _, _ in pieces]
         x = parts[0] if len(parts) == 1 else jnp.concatenate(parts, axis=0)
-        for order, j in enumerate((1, 2, 0)):
-            if n == 0:
-                w_in[order].wait()
-            made = jnp.dot(x, wv[j], preferred_element_type=jnp.float32)
-            made = made + bias[pl.ds(j, 1), :].astype(jnp.float32)
-            for g in range(heads):
-                cols = slice(g * HD, (g + 1) * HD)
-                piece = made[:, cols]
-                if j < 2:
-                    mean_sq = jnp.mean(piece * piece, axis=-1, keepdims=True)
-                    piece = piece * lax.rsqrt(mean_sq + 1e-06) * gains[pl.ds(j, 1), :]
-                piece = piece.astype(jnp.bfloat16)
-                if j == 0:
-                    at = 0
-                    for _, _, rows, block, start in pieces:
-                        qb[block, start : start + rows, cols] = piece[at : at + rows]
-                        at += rows
-                else:
-                    off = (j - 1) * width + g * HD
-                    kv[1, key_rows(n, c), off : off + HD] = piece
-            if j == 2:
-                kv_copy(1, 2, n, down, 2).start()
-                kv_copy(1, 0, n, up, 1).start()
-                kv_copy(1, 1, n, partner, 0).start()
+        def normed(piece, j):
+            mean_sq = jnp.mean(piece * piece, axis=-1, keepdims=True)
+            return piece * lax.rsqrt(mean_sq + 1e-06) * gains[j : j + 1, :]
+
+        def bias_of(j):
+            return bias[j : j + 1, :].astype(jnp.float32)
+
+        if n == 0:
+            w_in[0].wait()
+            w_in[1].wait()
+        both = jnp.concatenate([wv[1], wv[2]], axis=1)
+        made = jnp.dot(x, both, preferred_element_type=jnp.float32)
+        made = made + jnp.concatenate([bias_of(1), bias_of(2)], axis=1)
+        for g in range(2 * heads):
+            piece = made[:, g * HD : (g + 1) * HD]
+            if g < heads:
+                piece = normed(piece, 1)
+            kv[1, key_rows(n, c), g * HD : (g + 1) * HD] = piece.astype(jnp.bfloat16)
+        kv_copy(1, 2, n, down, 2).start()
+        kv_copy(1, 0, n, up, 1).start()
+        kv_copy(1, 1, n, partner, 0).start()
+        if n == 0:
+            w_in[2].wait()
+        made = jnp.dot(x, wv[0], preferred_element_type=jnp.float32) + bias_of(0)
+        for g in range(heads):
+            cols = slice(g * HD, (g + 1) * HD)
+            piece = normed(made[:, cols], 0).astype(jnp.bfloat16)
+            at = 0
+            for _, _, rows, block, start in pieces:
+                qb[block, start : start + rows, cols] = piece[at : at + rows]
+                at += rows
 
     def relay(n):
         kv_wait(0, n, c, 1)
@@ -202,35 +210,39 @@
 
     acc[...] = jnp.zeros_like(acc)
 
-    segments = {
-        0: [(chunk, 0, 0), (chunk, 0, 1)],
-        1: [(half, 1 - mate_left, 0), (half, mate_left, 0), (half, 1 - mate_left, 1), (half, mate_left, 1)],
-        3: [(half, 1, 0), (half, 1, 1)],
-    }
-    segments[2] = segments[1]
-    segments[4] = segments[3]
-
-    def attend(block, tile, f, group):
-        base = tile * 12 + f * 4
-        live = jnp.concatenate(
-            [
-                jnp.full((rows, HD), mask[base + kt * 2 + core], jnp.float32)
-                for n in group
-                for rows, kt, core in segments[n]
-            ],
-            axis=0,
-        ).astype(jnp.bfloat16)
-        keys = slice(batches[group[0]][0], batches[group[0]][0] + live.shape[0])
+    mixed = [(half, 1 - mate_left), (half, mate_left)]
+    segments = [[(chunk, 0)], mixed, mixed, [(2 * part, 1)], [(2 * rest, 1)]]
+
+    def attend(block, count, tile, groups):
+        spans = []
+        for f, group in groups:
+            base = tile * 12 + f * 4
+            live = jnp.concatenate(
+                [
+                    jnp.full((rows, HD), mask[base + kt * 2 + core], jnp.float32)
+                    for n in group
+                    for core in range(2)
+                    for rows, kt in segments[n]
+                ],
+                axis=0,
+            ).astype(jnp.bfloat16)
+            first = batches[group[0]][0]
+            spans.append((f, slice(first, first + live.shape[0]), live))
+        rows = pl.ds(block, count)
         for g in range(heads):
-            qh = qb[block, :, g * HD : (g + 1) * HD]
-            kh = kv[f, keys, g * HD : (g + 1) * HD]
-            vh = kv[f, keys, width + g * HD : width + (g + 1) * HD]
-            score = lax.dot_general(
-                qh, kh, (((1,), (1,)), ((), ())), preferred_element_type=jnp.float32
-            )
-            w = jnp.exp(score * HD ** (-0.5)).astype(jnp.bfloat16)
-            ext = jnp.concatenate([vh * live, live], axis=1)
-            acc[block, g] += jnp.dot(w, ext, preferred_element_type=jnp.float32)
+            qh = qb[rows, :, g * HD : (g + 1) * HD].reshape(count * chunk, HD)
+            added = None
+            for f, keys, live in spans:
+                kh = kv[f, keys, g * HD : (g + 1) * HD]
+                vh = kv[f, keys, width + g * HD : width + (g + 1) * HD]
+                score = lax.dot_general(
+                    qh, kh, (((1,), (1,)), ((), ())), preferred_element_type=jnp.float32
+                )
+                w = jnp.exp(score * HD ** (-0.5)).astype(jnp.bfloat16)
+                ext = jnp.concatenate([vh * live, live], axis=1)
+                term = jnp.dot(w, ext, preferred_element_type=jnp.float32)
+                added = term if added is None else added + term
+            acc[rows, g] += added.reshape(count, chunk, 2 * HD)
 
     def finish(block):
         for g in range(heads):
@@ -284,7 +296,7 @@
             far(0)
             far(1)
 
-        attend(0, 0, lax.rem(2 * i + 1, 3), (0, 1))
+        attend(0, 1, 0, [(lax.rem(2 * i + 1, 3), (0, 1))])
         return carry
 
     lax.fori_loop(0, 3, own_first, 0)
@@ -293,33 +305,21 @@
     project(2)
 
     def neighbours_first(i, carry):
-        block = 1 + lax.div(i, 3)
-        attend(block, lax.div(block, 2), lax.rem(i, 3), (0, 1))
+        attend(1 + i, 1, i, [(f, (0, 1)) for f in range(3)])
         return carry
 
-    lax.fori_loop(0, 6, neighbours_first, 0)
-    hid_wait(3, 0, quarter, 2)
-    hid_wait(3, 3 * quarter, quarter, 6)
+    lax.fori_loop(0, 2, neighbours_first, 0)
+    hid_wait(3, 0, part, 2)
+    hid_wait(3, chunk - part, part, 6)
     project(3)
     relay(2)
     near(2)
     near(3)
-
-    def own_second(i, carry):
-        attend(i, lax.div(i, 2), 1, (2, 3))
-        return carry
-
-    lax.fori_loop(0, 3, own_second, 0)
-    relay(3)
-    hid_wait(3, quarter, quarter, 3)
-    hid_wait(3, 2 * quarter, quarter, 7)
+    attend(0, 2, 0, [(1, (2, 3))])
+    hid_wait(3, part, rest, 3)
+    hid_wait(3, half, rest, 7)
     project(4)
-
-    def opposite_first(i, carry):
-        attend(3, 1, i, (0, 1))
-        return carry
-
-    lax.fori_loop(0, 3, opposite_first, 0)
+    attend(3, 1, 1, [(f, (0, 1)) for f in range(3)])
     keep = [pltpu.make_async_copy(qb, q_out, x_sem.at[5])]
     at = 0
     for n, (_, rows, _) in enumerate(batches):
@@ -327,49 +327,45 @@
         at += rows
     for copy in keep:
         copy.start()
+    relay(3)
+    attend(2, 2, 1, [(1, (2, 3))])
     far(2)
     far(3)
 
     def second(i, carry):
-        new = lax.div(i + 8, 9)
-        block = 3 - new * lax.div(i + 1 - 2 * new + (1 - new), 2)
-        attend(block, lax.div(block, 2), (1 - new) + new * 2 * lax.rem(i, 2), (2, 3))
+        @pl.when(i == 1)
+        def _():
+            relay(4)
+
+        attend(2 - 2 * i, 2, 1 - i, [(0, (2, 3)), (2, (2, 3))])
         return carry
 
-    lax.fori_loop(0, 9, second, 0)
-    relay(4)
+    lax.fori_loop(0, 2, second, 0)
     near(4)
+    far(4)
 
     def last(i, carry):
-        new = lax.div(i + 8, 12)
-
-        @pl.when(i == 4)
-        def _():
-            far(4)
-
-        block = (1 - new) * i + new * (5 - lax.div(i, 2))
-        attend(block, lax.div(block, 2), (1 - new) + new * 2 * lax.rem(i, 2), (4,))
-
-        @pl.when((i >= 4) & (lax.rem(i, 2) == 1))
-        def _():
-            finish(block)
-
-        @pl.when(i == 5)
+        attend(2 - 2 * i, 2, 1 - i, [(f, (4,)) for f in range(3)])
+        finish(3 - 2 * i)
+
+        @pl.when(i == 0)
         def _():
             out_sends[0].start()
             out_sends[1].start()
 
-        @pl.when(i == 7)
+        finish(2 - 2 * i)
+
+        @pl.when(i == 0)
         def _():
             out_sends[2].start()
 
-        @pl.when(i == 9)
+        @pl.when(i == 1)
         def _():
             out_sends[3].start()
 
         return carry
 
-    lax.fori_loop(0, 12, last, 0)
+    lax.fori_loop(0, 2, last, 0)
     own_out.start()
     for k in range(2):
         ref = passing.at[k]
@@ -457,7 +453,7 @@
     chunk, width = query.shape[1:]
     heads = width // HD
     rows = 2 * TILE
-    half, quarter = chunk // 2, chunk // 4
+    half, part = chunk // 2, chunk // 3
 
     def in_order(own, right, opposite, left):
         around = jnp.concatenate([own, right, opposite, left] * 2, axis=0)
@@ -471,7 +467,7 @@
     current = in_order(
         key_value[:chunk],
         jnp.concatenate([two[half:], one[half:]], axis=0),
-        jnp.concatenate([opp[:quarter], opp[half:], opp[quarter:half]], axis=0),
+        jnp.concatenate([opp[:part], opp[2 * part :], opp[part : 2 * part]], axis=0),
         jnp.concatenate([one[:half], two[:half]], axis=0),
     )
     lists = lax.dynamic_slice_in_dim(tile_lists, place * 2, 2, 0)

time: 77.3 us -> 72 us (0.931)
  Pallas kernels: 75.6 us -> 70.4 us
    pallas_call x1, Pallas kernels: 75.6 us -> 70.4 us  [window_attention(): pl.pallas_call(functools.partial(kernel, sizes), out_shape=(jax.ShapeDtyp...]
where the time goes in v3:
time: 72 us; the launch traced here: 71.8 us
  Pallas kernels  70.4 us (98%)
  local copies, waits for them, and re-layouts  0.82 us (1%)
    pallas_call x1, Pallas kernels, window_attention(): pl.pallas_call(functools.partial(kernel, sizes), out_shape=(jax.ShapeDtyp...  70.4 us

profile of v3, /device:TPU:1, one launch (start us, length us, event | category | flops | bytes accessed | tf_op | source)
XLA Modules:
  0.0 71.8 jit_solution(2024496223015506834)
XLA Ops:
  0.0 0.0 copy-start.8
  0.0 0.0 copy-start.9
  0.0 70.4 %shard_map.66 = (bf16[192,1536]{1,0:T(8,128)(2,1)S(1)}, bf16[4,192,384]{2,1,0:T(8,128)(2,1)S(1)}, bf16[768,768]{1,0:T(8,128)(2,1)S(1)}, s32[1,1]{1,0:T(1,128)}) custom-call(bf16[192,3072]{1,0:T(8,128)(2,1)} %hidden.1, bf16[3,3072,384]{2,1,0:T(8,128)(2,1)} %weight.1, bf16[3,384]{1,0:T(4,128)(2,1)} %bias.1, f32[2,128]{1,0:T(2,128)} %gains.1, ...), custom_call_target="tpu_custom_call" | custom-call | tf_op jit(solution)/shard_map/pallas_call | solution.py:411
  71.0 0.0 copy-done.8
  71.0 0.0 copy-done.9
  71.0 0.8 %copy.61 = bf16[192,1536]{1,0:T(8,128)(2,1)} copy(bf16[192,1536]{1,0:T(8,128)(2,1)S(1)} %get-tuple-element.231) | data formatting | bytes 1179648
  (1 shorter events, 0.0 us)
Async XLA Ops:
  0.0 71.0 %copy-start.8 = (s32[32,12]{0,1:T(8,128)S(1)}, s32[32,12]{0,1:T(8,128)}, u32[]{:S(2)}) copy-start(s32[32,12]{0,1:T(8,128)} %param.14) | copy-start | bytes 4612
  0.0 71.0 %copy-start.9 = (s32[32]{0:T(128)S(1)}, s32[32]{0:T(128)}, u32[]{:S(2)}) copy-start(s32[32]{0:T(128)} %counts.1) | copy-start | bytes 388

commit v4 on v3

--- a/solution.py
+++ b/solution.py
@@ -14,10 +14,11 @@
 
 def kernel(
     sizes,
-    hidden, weight, bias, gains, lists, counts,
+    hidden, weight, bias_in, gains_in, lists_in, counts_in,
     out, q_out, kv_out, flag_out,
     hid, wv, qb, kv, acc, ob, passing, flags, mask,
-    own_sem, w_sem, hs_sem, hr_sem, ks_sem, kr_sem, os_sem, or_sem, fs_sem, fr_sem, x_sem,
+    bias, gains, lists, counts,
+    own_sem, w_sem, hs_sem, hr_sem, ks_sem, kr_sem, os_sem, or_sem, fs_sem, fr_sem, x_sem, s_sem,
 ):
     n_blk, n_dp, heads, slots, n_tiles = sizes
     chunk = hid.shape[1]
@@ -41,22 +42,30 @@
     partner = b + 1 - 2 * c
     up = lax.rem(b + 2, n_blk)
     down = lax.rem(b + n_blk - 2, n_blk)
-    dps = [lax.rem(d + i, n_dp) for i in range(1, n_dp)]
-
+    d_up = lax.rem(d + 1, n_dp)
+    d_down = lax.rem(d + n_dp - 1, n_dp)
+
+    barrier = pltpu.get_barrier_semaphore()
+    for p in (right, left):
+        pl.semaphore_signal(barrier, inc=1, device_id={"head": p}, device_id_type=MESH)
+    for p in (up, down, partner):
+        pl.semaphore_signal(barrier, inc=1, device_id={"blk": p}, device_id_type=MESH)
+    for p in (d_up, d_down):
+        pl.semaphore_signal(barrier, inc=1, device_id={"dp": p}, device_id_type=MESH)
     own_in = pltpu.make_async_copy(hidden, hid.at[0], own_sem)
     own_in.start()
     w_in = [pltpu.make_async_copy(weight.at[j], wv.at[j], w_sem.at[j]) for j in (1, 2, 0)]
     for copy in w_in:
         copy.start()
-
-    barrier = pltpu.get_barrier_semaphore()
-    for p in (right, opp, left):
-        pl.semaphore_signal(barrier, inc=1, device_id={"head": p}, device_id_type=MESH)
-    for p in (partner, up, down):
-        pl.semaphore_signal(barrier, inc=1, device_id={"blk": p}, device_id_type=MESH)
-    for p in dps:
-        pl.semaphore_signal(barrier, inc=1, device_id={"dp": p}, device_id_type=MESH)
-    pl.semaphore_wait(barrier, 6 + len(dps))
+    small = [
+        pltpu.make_async_copy(src, dst, s_sem.at[k])
+        for k, (src, dst) in enumerate(
+            ((bias_in, bias), (gains_in, gains), (lists_in, lists), (counts_in, counts))
+        )
+    ]
+    for copy in small:
+        copy.start()
+    pl.semaphore_wait(barrier, 7)
 
     def hid_send(src, slot, start, rows, to, k):
         return pltpu.make_async_remote_copy(
@@ -165,7 +174,11 @@
         kv_wait(2, n, 1 - c, 4)
 
     own_in.wait()
+    small[0].wait()
+    small[1].wait()
     project(0)
+    small[2].wait()
+    small[3].wait()
 
     def check_row(t, bad):
         n = counts[t]
@@ -176,7 +189,7 @@
         return bad
 
     bad = lax.fori_loop(0, n_tiles, check_row, jnp.int32(0))
-    flags[d] = jnp.full(flags.shape[1:], bad, jnp.int32)
+    flags[0] = jnp.full(flags.shape[1:], bad, jnp.int32)
 
     def mask_entry(i, carry):
         q = i // 12
@@ -194,19 +207,23 @@
 
     lax.fori_loop(0, 24, mask_entry, 0)
 
-    def flag_send(i, to):
+    def flag_send(src, dst, to, k):
         return pltpu.make_async_remote_copy(
-            src_ref=flags.at[d],
-            dst_ref=flags.at[d],
-            send_sem=fs_sem.at[i],
-            recv_sem=fr_sem.at[i],
+            src_ref=flags.at[src],
+            dst_ref=flags.at[dst],
+            send_sem=fs_sem.at[k],
+            recv_sem=fr_sem.at[k],
             device_id={"dp": to},
             device_id_type=MESH,
         )
 
-    flag_sends = [flag_send(i, p) for i, p in enumerate(dps)]
-    for copy in flag_sends:
-        copy.start()
+    flag_sends = [flag_send(0, 1, d_up, 0), flag_send(0, 2, d_down, 1), flag_send(3, 4, d_up, 2)]
+    flag_sends[0].start()
+    flag_sends[1].start()
+
+    def flag_wait(dst, k):
+        ref = flags.at[dst]
+        pltpu.make_async_copy(ref, ref, fr_sem.at[k]).wait()
 
     acc[...] = jnp.zeros_like(acc)
 
@@ -281,11 +298,9 @@
     hops[7].start()
     relay(0)
     project(1)
-    for i in range(n_dp - 1):
-        src = lax.rem(d + n_dp - 1 - i, n_dp)
-        ref = flags.at[src]
-        pltpu.make_async_copy(ref, ref, fr_sem.at[i]).wait()
-    flag_out[...] = jnp.max(flags[:, 0:1, 0:1], axis=0)
+    flag_wait(1, 0)
+    flags[3] = jnp.maximum(flags[0], flags[1])
+    flag_sends[2].start()
     near(0)
     near(1)
 
@@ -300,6 +315,10 @@
         return carry
 
     lax.fori_loop(0, 3, own_first, 0)
+    flag_wait(2, 1)
+    flag_wait(4, 2)
+    seen = jnp.maximum(jnp.maximum(flags[2], flags[3]), flags[4])
+    flag_out[...] = seen[0:1, 0:1]
     hid_wait(1, half, half, 1)
     hid_wait(2, 0, half, 5)
     project(2)
@@ -314,8 +333,8 @@
     project(3)
     relay(2)
     near(2)
-    near(3)
-    attend(0, 2, 0, [(1, (2, 3))])
+    far(2)
+    attend(0, 2, 0, [(f, (2,)) for f in range(3)])
     hid_wait(3, part, rest, 3)
     hid_wait(3, half, rest, 7)
     project(4)
@@ -328,16 +347,13 @@
     for copy in keep:
         copy.start()
     relay(3)
-    attend(2, 2, 1, [(1, (2, 3))])
-    far(2)
+    attend(2, 2, 1, [(f, (2,)) for f in range(3)])
+    near(3)
     far(3)
+    relay(4)
 
     def second(i, carry):
-        @pl.when(i == 1)
-        def _():
-            relay(4)
-
-        attend(2 - 2 * i, 2, 1 - i, [(0, (2, 3)), (2, (2, 3))])
+        attend(2 - 2 * i, 2, 1 - i, [(f, (3,)) for f in range(3)])
         return carry
 
     lax.fori_loop(0, 2, second, 0)
@@ -406,7 +422,6 @@
     sizes = (n_blk, n_dp, heads, slots, n_tiles)
     hbm = pl.BlockSpec(memory_space=pl.ANY)
     vmem = pl.BlockSpec(memory_space=pltpu.VMEM)
-    smem = pl.BlockSpec(memory_space=pltpu.SMEM)
     dma = pltpu.SemaphoreType.DMA
     return pl.pallas_call(
         functools.partial(kernel, sizes),
@@ -416,7 +431,7 @@
             jax.ShapeDtypeStruct((4 * chunk, 2 * width), jnp.bfloat16),
             jax.ShapeDtypeStruct((1, 1), jnp.int32),
         ),
-        in_specs=[hbm, hbm, vmem, vmem, smem, smem],
+        in_specs=[hbm] * 6,
         out_specs=(hbm, hbm, hbm, vmem),
         scratch_shapes=[
             pltpu.VMEM((4, chunk, depth), jnp.bfloat16),
@@ -426,8 +441,12 @@
             pltpu.VMEM((4, heads, chunk, 2 * HD), jnp.float32),
             pltpu.VMEM((4, chunk, width), jnp.bfloat16),
             pltpu.VMEM((2, chunk // 2, width), jnp.bfloat16),
-            pltpu.VMEM((n_dp, 8, 128), jnp.int32),
+            pltpu.VMEM((5, 8, 128), jnp.int32),
             pltpu.SMEM((24,), jnp.float32),
+            pltpu.VMEM(bias.shape, bias.dtype),
+            pltpu.VMEM(gains.shape, gains.dtype),
+            pltpu.SMEM(lists.shape, lists.dtype),
+            pltpu.SMEM(counts.shape, counts.dtype),
             dma,
             dma((3,)),
             dma((8,)),
@@ -436,9 +455,10 @@
             dma((5, 5)),
             dma((6,)),
             dma((6,)),
-            dma((n_dp - 1,)),
-            dma((n_dp - 1,)),
+            dma((3,)),
+            dma((3,)),
             dma((6,)),
+            dma((4,)),
         ],
         compiler_params=pltpu.CompilerParams(
             collective_id=0, has_side_effects=True, vmem_limit_bytes=60 * 1024 * 1024

time: 72 us -> 71.9 us (level)
  no operation moved by 1% of the time
where the time goes in v4:
time: 71.9 us; the launch traced here: 71.8 us
  Pallas kernels  70.4 us (98%)
  local copies, waits for them, and re-layouts  0.82 us (1%)
    pallas_call x1, Pallas kernels, window_attention(): pl.pallas_call(functools.partial(kernel, sizes), out_shape=(jax.ShapeDtyp...  70.4 us

profile of v4, /device:TPU:1, one launch (start us, length us, event | category | flops | bytes accessed | tf_op | source)
XLA Modules:
  0.0 71.8 jit_solution(1407826401422542699)
XLA Ops:
  0.0 0.0 copy-start.8
  0.0 0.0 copy-start.9
  0.0 70.4 %shard_map.66 = (bf16[192,1536]{1,0:T(8,128)(2,1)S(1)}, bf16[4,192,384]{2,1,0:T(8,128)(2,1)S(1)}, bf16[768,768]{1,0:T(8,128)(2,1)S(1)}, s32[1,1]{1,0:T(1,128)}) custom-call(bf16[192,3072]{1,0:T(8,128)(2,1)} %hidden.1, bf16[3,3072,384]{2,1,0:T(8,128)(2,1)} %weight.1, bf16[3,384]{1,0:T(4,128)(2,1)} %bias_in.1, f32[2,128]{1,0:T(2,128)} %gains_in.1, ...), custom_call_target="tpu_custom_call" | custom-call | tf_op jit(solution)/shard_map/pallas_call | solution.py:426
  71.0 0.0 copy-done.8
  71.0 0.0 copy-done.9
  71.0 0.8 %copy.61 = bf16[192,1536]{1,0:T(8,128)(2,1)} copy(bf16[192,1536]{1,0:T(8,128)(2,1)S(1)} %get-tuple-element.231) | data formatting | bytes 1179648
  (1 shorter events, 0.0 us)
Async XLA Ops:
  0.0 71.0 %copy-start.8 = (s32[32,12]{0,1:T(8,128)S(1)}, s32[32,12]{0,1:T(8,128)}, u32[]{:S(2)}) copy-start(s32[32,12]{0,1:T(8,128)} %param.14) | copy-start | bytes 4612
  0.0 71.0 %copy-start.9 = (s32[32]{0:T(128)S(1)}, s32[32]{0:T(128)}, u32[]{:S(2)}) copy-start(s32[32]{0:T(128)} %counts_in.1) | copy-start | bytes 388

commit v5 on v4

--- a/solution.py
+++ b/solution.py
@@ -230,7 +230,7 @@
     mixed = [(half, 1 - mate_left), (half, mate_left)]
     segments = [[(chunk, 0)], mixed, mixed, [(2 * part, 1)], [(2 * rest, 1)]]
 
-    def attend(block, count, tile, groups):
+    def attend(block, count, tile, groups, joined=False):
         spans = []
         for f, group in groups:
             base = tile * 12 + f * 4
@@ -248,15 +248,23 @@
         rows = pl.ds(block, count)
         for g in range(heads):
             qh = qb[rows, :, g * HD : (g + 1) * HD].reshape(count * chunk, HD)
+            pieces = [
+                (
+                    kv[f, keys, g * HD : (g + 1) * HD],
+                    jnp.concatenate(
+                        [kv[f, keys, width + g * HD : width + (g + 1) * HD] * live, live], axis=1
+                    ),
+                )
+                for f, keys, live in spans
+            ]
+            if joined:
+                pieces = [tuple(jnp.concatenate(part, axis=0) for part in zip(*pieces))]
             added = None
-            for f, keys, live in spans:
-                kh = kv[f, keys, g * HD : (g + 1) * HD]
-                vh = kv[f, keys, width + g * HD : width + (g + 1) * HD]
+            for kh, ext in pieces:
                 score = lax.dot_general(
                     qh, kh, (((1,), (1,)), ((), ())), preferred_element_type=jnp.float32
                 )
                 w = jnp.exp(score * HD ** (-0.5)).astype(jnp.bfloat16)
-                ext = jnp.concatenate([vh * live, live], axis=1)
                 term = jnp.dot(w, ext, preferred_element_type=jnp.float32)
                 added = term if added is None else added + term
             acc[rows, g] += added.reshape(count, chunk, 2 * HD)
@@ -334,7 +342,7 @@
     relay(2)
     near(2)
     far(2)
-    attend(0, 2, 0, [(f, (2,)) for f in range(3)])
+    attend(0, 2, 0, [(f, (2,)) for f in range(3)], True)
     hid_wait(3, part, rest, 3)
     hid_wait(3, half, rest, 7)
     project(4)
@@ -347,41 +355,23 @@
     for copy in keep:
         copy.start()
     relay(3)
-    attend(2, 2, 1, [(f, (2,)) for f in range(3)])
+    attend(2, 2, 1, [(f, (2,)) for f in range(3)], True)
     near(3)
     far(3)
     relay(4)
-
-    def second(i, carry):
-        attend(2 - 2 * i, 2, 1 - i, [(f, (3,)) for f in range(3)])
-        return carry
-
-    lax.fori_loop(0, 2, second, 0)
+    attend(2, 2, 1, [(f, (3,)) for f in range(3)], True)
     near(4)
     far(4)
-
-    def last(i, carry):
-        attend(2 - 2 * i, 2, 1 - i, [(f, (4,)) for f in range(3)])
-        finish(3 - 2 * i)
-
-        @pl.when(i == 0)
-        def _():
-            out_sends[0].start()
-            out_sends[1].start()
-
-        finish(2 - 2 * i)
-
-        @pl.when(i == 0)
-        def _():
-            out_sends[2].start()
-
-        @pl.when(i == 1)
-        def _():
-            out_sends[3].start()
-
-        return carry
-
-    lax.fori_loop(0, 2, last, 0)
+    attend(2, 2, 1, [(f, (4,)) for f in range(3)], True)
+    finish(3)
+    out_sends[0].start()
+    out_sends[1].start()
+    finish(2)
+    out_sends[2].start()
+    attend(0, 2, 0, [(f, (3, 4)) for f in range(3)], True)
+    finish(1)
+    out_sends[3].start()
+    finish(0)
     own_out.start()
     for k in range(2):
         ref = passing.at[k]

time: 71.9 us -> 69.3 us (0.964)
  Pallas kernels: 70.4 us -> 67.8 us
    pallas_call x1, Pallas kernels: 70.4 us -> 67.8 us  [window_attention(): pl.pallas_call(functools.partial(kernel, sizes), out_shape=(jax.ShapeDtyp...]
where the time goes in v5:
time: 69.3 us; the launch traced here: 69.2 us
  Pallas kernels  67.8 us (98%)
  local copies, waits for them, and re-layouts  0.82 us (1%)
    pallas_call x1, Pallas kernels, window_attention(): pl.pallas_call(functools.partial(kernel, sizes), out_shape=(jax.ShapeDtyp...  67.8 us

profile of v5, /device:TPU:1, one launch (start us, length us, event | category | flops | bytes accessed | tf_op | source)
XLA Modules:
  0.0 69.2 jit_solution(17621683101467842520)
XLA Ops:
  0.0 0.0 copy-start.8
  0.0 0.0 copy-start.9
  0.0 67.8 %shard_map.66 = (bf16[192,1536]{1,0:T(8,128)(2,1)S(1)}, bf16[4,192,384]{2,1,0:T(8,128)(2,1)S(1)}, bf16[768,768]{1,0:T(8,128)(2,1)S(1)}, s32[1,1]{1,0:T(1,128)}) custom-call(bf16[192,3072]{1,0:T(8,128)(2,1)} %hidden.1, bf16[3,3072,384]{2,1,0:T(8,128)(2,1)} %weight.1, bf16[3,384]{1,0:T(4,128)(2,1)} %bias_in.1, f32[2,128]{1,0:T(2,128)} %gains_in.1, ...), custom_call_target="tpu_custom_call" | custom-call | tf_op jit(solution)/shard_map/pallas_call | solution.py:416
  68.3 0.0 copy-done.8
  68.4 0.0 copy-done.9
  68.4 0.8 %copy.61 = bf16[192,1536]{1,0:T(8,128)(2,1)} copy(bf16[192,1536]{1,0:T(8,128)(2,1)S(1)} %get-tuple-element.231) | data formatting | bytes 1179648
  (1 shorter events, 0.0 us)
Async XLA Ops:
  0.0 68.4 %copy-start.8 = (s32[32,12]{0,1:T(8,128)S(1)}, s32[32,12]{0,1:T(8,128)}, u32[]{:S(2)}) copy-start(s32[32,12]{0,1:T(8,128)} %param.14) | copy-start | bytes 4612
  0.0 68.4 %copy-start.9 = (s32[32]{0:T(128)S(1)}, s32[32]{0:T(128)}, u32[]{:S(2)}) copy-start(s32[32]{0:T(128)} %counts_in.1) | copy-start | bytes 388

commit v6 on v5

--- a/solution.py
+++ b/solution.py
@@ -336,13 +336,16 @@
         return carry
 
     lax.fori_loop(0, 2, neighbours_first, 0)
+    near(2)
+    attend(0, 2, 0, [(1, (2,))])
+    attend(2, 1, 1, [(1, (2,))])
     hid_wait(3, 0, part, 2)
     hid_wait(3, chunk - part, part, 6)
     project(3)
     relay(2)
-    near(2)
     far(2)
-    attend(0, 2, 0, [(f, (2,)) for f in range(3)], True)
+    attend(0, 2, 0, [(0, (2,)), (2, (2,))], True)
+    attend(2, 1, 1, [(0, (2,)), (2, (2,))], True)
     hid_wait(3, part, rest, 3)
     hid_wait(3, half, rest, 7)
     project(4)
@@ -355,7 +358,7 @@
     for copy in keep:
         copy.start()
     relay(3)
-    attend(2, 2, 1, [(f, (2,)) for f in range(3)], True)
+    attend(3, 1, 1, [(f, (2,)) for f in range(3)], True)
     near(3)
     far(3)
     relay(4)

time: 69.3 us -> 68.8 us (level)
  no operation moved by 1% of the time
where the time goes in v6:
time: 68.8 us; the launch traced here: 68.7 us
  Pallas kernels  67.3 us (98%)
  local copies, waits for them, and re-layouts  0.82 us (1%)
    pallas_call x1, Pallas kernels, window_attention(): pl.pallas_call(functools.partial(kernel, sizes), out_shape=(jax.ShapeDtyp...  67.3 us

profile of v6, /device:TPU:1, one launch (start us, length us, event | category | flops | bytes accessed | tf_op | source)
XLA Modules:
  0.0 68.7 jit_solution(1655382283786179669)
XLA Ops:
  0.0 0.0 copy-start.8
  0.0 0.0 copy-start.9
  0.0 67.3 %shard_map.66 = (bf16[192,1536]{1,0:T(8,128)(2,1)S(1)}, bf16[4,192,384]{2,1,0:T(8,128)(2,1)S(1)}, bf16[768,768]{1,0:T(8,128)(2,1)S(1)}, s32[1,1]{1,0:T(1,128)}) custom-call(bf16[192,3072]{1,0:T(8,128)(2,1)} %hidden.1, bf16[3,3072,384]{2,1,0:T(8,128)(2,1)} %weight.1, bf16[3,384]{1,0:T(4,128)(2,1)} %bias_in.1, f32[2,128]{1,0:T(2,128)} %gains_in.1, ...), custom_call_target="tpu_custom_call" | custom-call | tf_op jit(solution)/shard_map/pallas_call | solution.py:419
  67.9 0.0 copy-done.8
  67.9 0.0 copy-done.9
  67.9 0.8 %copy.61 = bf16[192,1536]{1,0:T(8,128)(2,1)} copy(bf16[192,1536]{1,0:T(8,128)(2,1)S(1)} %get-tuple-element.231) | data formatting | bytes 1179648
  (1 shorter events, 0.0 us)
Async XLA Ops:
  0.0 67.9 %copy-start.8 = (s32[32,12]{0,1:T(8,128)S(1)}, s32[32,12]{0,1:T(8,128)}, u32[]{:S(2)}) copy-start(s32[32,12]{0,1:T(8,128)} %param.14) | copy-start | bytes 4612
  0.0 67.9 %copy-start.9 = (s32[32]{0:T(128)S(1)}, s32[32]{0:T(128)}, u32[]{:S(2)}) copy-start(s32[32]{0:T(128)} %counts_in.1) | copy-start | bytes 388

commit v7 on v6

--- a/solution.py
+++ b/solution.py
@@ -355,8 +355,6 @@
     for n, (_, rows, _) in enumerate(batches):
         keep.append(pltpu.make_async_copy(kv.at[1, key_rows(n, c)], kv_out.at[pl.ds(at, rows)], x_sem.at[n]))
         at += rows
-    for copy in keep:
-        copy.start()
     relay(3)
     attend(3, 1, 1, [(f, (2,)) for f in range(3)], True)
     near(3)
@@ -376,6 +374,8 @@
     out_sends[3].start()
     finish(0)
     own_out.start()
+    for copy in keep:
+        copy.start()
     for k in range(2):
         ref = passing.at[k]
         pltpu.make_async_copy(ref, ref, or_sem.at[k]).wait()

time: 68.8 us -> 68.8 us (level)
  no operation moved by 1% of the time
where the time goes in v7:
time: 68.8 us; the launch traced here: 68.7 us
  Pallas kernels  67.3 us (98%)
  local copies, waits for them, and re-layouts  0.82 us (1%)
    pallas_call x1, Pallas kernels, window_attention(): pl.pallas_call(functools.partial(kernel, sizes), out_shape=(jax.ShapeDtyp...  67.3 us

profile of v7, /device:TPU:1, one launch (start us, length us, event | category | flops | bytes accessed | tf_op | source)
XLA Modules:
  0.0 68.7 jit_solution(4926103340112117266)
XLA Ops:
  0.0 0.0 copy-start.8
  0.0 0.0 copy-start.9
  0.0 67.3 %shard_map.66 = (bf16[192,1536]{1,0:T(8,128)(2,1)S(1)}, bf16[4,192,384]{2,1,0:T(8,128)(2,1)S(1)}, bf16[768,768]{1,0:T(8,128)(2,1)S(1)}, s32[1,1]{1,0:T(1,128)}) custom-call(bf16[192,3072]{1,0:T(8,128)(2,1)} %hidden.1, bf16[3,3072,384]{2,1,0:T(8,128)(2,1)} %weight.1, bf16[3,384]{1,0:T(4,128)(2,1)} %bias_in.1, f32[2,128]{1,0:T(2,128)} %gains_in.1, ...), custom_call_target="tpu_custom_call" | custom-call | tf_op jit(solution)/shard_map/pallas_call | solution.py:419
  67.9 0.0 copy-done.8
  67.9 0.0 copy-done.9
  67.9 0.8 %copy.61 = bf16[192,1536]{1,0:T(8,128)(2,1)} copy(bf16[192,1536]{1,0:T(8,128)(2,1)S(1)} %get-tuple-element.231) | data formatting | bytes 1179648
  (1 shorter events, 0.0 us)
Async XLA Ops:
  0.0 67.9 %copy-start.8 = (s32[32,12]{0,1:T(8,128)S(1)}, s32[32,12]{0,1:T(8,128)}, u32[]{:S(2)}) copy-start(s32[32,12]{0,1:T(8,128)} %param.14) | copy-start | bytes 4612
  0.0 67.9 %copy-start.9 = (s32[32]{0:T(128)S(1)}, s32[32]{0:T(128)}, u32[]{:S(2)}) copy-start(s32[32]{0:T(128)} %counts_in.1) | copy-start | bytes 388
